TPU v7x, 32 devices: a whole 2x2x4 slice. The times are simulated.
32 devices in a mesh: segment: 2 (over core), expert: 16 (over z, y, x).
Axes of the slice: x: 2, y: 2, z: 4, core: 2. Of those that a mesh axis runs over, the one named last changes fastest.
Arguments:
- rollout: bfloat16 [2048, 4096], P('expert', 'segment'), may hold values from -6 to 6
- norm_gain: bfloat16 [2, 4096], P('segment'), may hold values from 0.25 to 1.75
- router_first: bfloat16 [2, 4096, 28], P('segment')
- gain_second: bfloat16 [2, 4096], P('segment'), may hold values from 0.25 to 1.75
- router_second: bfloat16 [2, 4096, 28], P('segment')
- expert_ids: int32 [2048, 8], P('expert'), may hold values from 0 to 27, as said below
- copy_pick: int32 [2048, 8], P('expert'), may hold values from 0 to 5
- later_ids: int32 [2048, 8], P('expert'), may hold values from 0 to 27, all different within a row
- slot_table: int32 [32], replicated, may hold values from 0 to 27, as said below
- expert_in: bfloat16 [32, 4096, 1536], P(('segment', 'expert'))
- expert_out: bfloat16 [32, 768, 4096], P(('segment', 'expert'))
Outputs:
- states: bfloat16 [2, 2048, 4096], P('segment', 'expert')
- log_ratio: float32 [1024, 2], P('expert', 'segment')
Inputs may be any that keep to these rules, and one draw needn't show every extreme that they name: `expert_ids`: each row names 8 different experts. `slot_table`: every expert is held by one, two or three slots.
All inputs are finite; a program needn't handle non-finite values.
Results may differ from a plain program's by a relative error of at most 0.013.
The roundings to bfloat16 on the way count: a program that leaves them out, or rounds other values in their place, can miss the bound.
Values may be sent and summed in bfloat16 or wider, within the bound.
A program may use at most 192 MiB of HBM per device.

v0:
```python
import functools
import math

import jax
import jax.numpy as jnp
from jax import lax
from jax.experimental import pallas as pl
from jax.experimental.pallas import tpu as pltpu
from jax.sharding import PartitionSpec as P

LANES = 128
VMEM_BUDGET = 26 << 20
VMEM_LIMIT = 60 * 1024 * 1024
MESH = pl.DeviceIdType.MESH
INFO_ROWS = 16
FACTOR_ROW = 12


def grid_sides(count):
    outer = 1
    while outer**3 < count:
        outer *= 2
    rest = count // outer
    middle = 1
    while middle**2 < rest:
        middle *= 2
    return outer, middle, rest // middle


class Plan:
    def __init__(self, sides):
        logs = [side.bit_length() - 1 for side in sides]
        n_a, n_b, n_c = logs
        bits_c = list(range(n_c))
        bits_b = list(range(n_c, n_c + n_b))
        bits_a = list(range(n_c + n_b, n_c + n_b + n_a))
        self.count = n_a + n_b + n_c
        self.blocks = 1 << self.count
        self.leaf = (bits_c[0], bits_b[0])
        orders = (
            (bits_c + bits_a + bits_b, bits_c + bits_b + bits_a),
            (bits_b + bits_a + bits_c, bits_b + bits_c + bits_a),
        )
        self.rest = [[order[1:] for order in pair] for pair in orders]
        self.stages = self.count - 1

    def dims(self, which, order, done):
        used = [self.leaf[which]] + self.rest[which][order][:done]
        return [bit for bit in reversed(range(self.count)) if bit not in used]


def bit_of(index, bit):
    return (index // (1 << bit)) % 2


def flip(index, bit):
    return index + (1 << bit) * (1 - 2 * bit_of(index, bit))


def digits(value, count):
    return [(value // (1 << (count - 1 - i))) % 2 for i in range(count)]


def spread_index(value, bit, own):
    low = 1 << bit
    return (value // low) * (2 * low) + own * low + value % low


def remote(src, dst, send, recv, peer):
    return pltpu.make_async_remote_copy(
        src_ref=src,
        dst_ref=dst,
        send_sem=send,
        recv_sem=recv,
        device_id=peer,
        device_id_type=MESH,
    )


def run_stages(chunks, stages, after_first=None):
    depth = max(lag for lag, _ in stages)

    @pl.loop(0, chunks + depth)
    def _(step):
        for lag, stage in stages:

            @pl.when((step >= lag) & (step - lag < chunks))
            def _():
                stage(step - lag)

        if after_first is not None:

            @pl.when(step == 0)
            def _():
                after_first()


def by_parity(stage):
    def run(j):
        for which in range(2):

            @pl.when(j % 2 == which)
            def _():
                stage(which, j)

    return run


def return_kernel(plan, chunks, act, w_out, told, out, wts, ys, leaf, swapped, *rest):
    stages = plan.stages
    parts, arrived, sems = rest[:stages], rest[stages : 2 * stages], rest[2 * stages :]
    seg = lax.axis_index("segment")
    me = lax.axis_index("expert")
    side = plan.blocks // 2
    room = ys.shape[-2]
    wide = ys.shape[-1]
    slot_rows = plan.blocks * room
    tok_rows = out.shape[0]
    half_rows = tok_rows // 2
    mine = [bit_of(me, bit) for bit in range(plan.count)]

    barrier = pltpu.get_barrier_semaphore()
    friends = [(1 - seg, me)]
    friends += [(seg, flip(me, bit)) for bit in range(plan.count)]
    friends += [(1 - seg, flip(me, bit)) for bit in plan.leaf]
    for friend in friends:
        pl.semaphore_signal(barrier, inc=1, device_id=friend, device_id_type=MESH)
    pl.semaphore_wait(barrier, len(friends))

    def region(which, own):
        bit = plan.leaf[which]
        place = plan.count - 1 - bit
        return tuple(
            (mine[bit] if own else 1 - mine[bit]) if i == place else slice(None)
            for i in range(plan.count)
        )

    def first_copies(which, j):
        slot = j % 3
        nbr = flip(me, plan.leaf[which])
        sources = (
            (ys.at[(slot, 1) + region(which, False)], leaf.at[j, 0], (seg, nbr)),
            (ys.at[(slot, 0) + region(which, False)], leaf.at[j, 1], (1 - seg, nbr)),
            (ys.at[(slot, 0) + region(which, True)], swapped.at[j], (1 - seg, me)),
        )
        return [
            remote(src, dst, sems[0].at[slot, k], sems[1].at[j, k], peer)
            for k, (src, dst, peer) in enumerate(sources)
        ]

    def send(which, t, r, j):
        bit = plan.rest[which][r][t]
        dims = plan.dims(which, r, t)
        index = tuple(1 - mine[d] if d == bit else slice(None) for d in dims)
        if t == 0:
            src = parts[0].at[(j % 2,) + index + (pl.ds(r * half_rows, half_rows),)]
        else:
            src = parts[t].at[(j % 2, r) + index]
        return remote(
            src,
            arrived[t].at[j, r],
            sems[2 + 2 * t].at[j % 2, r],
            sems[3 + 2 * t].at[j, r],
            (seg, flip(me, bit)),
        )

    def project(which, j):
        columns = pl.ds(pl.multiple_of(j * wide, wide), wide)
        blocks = (2,) * plan.count
        for section in range(2):
            result = jnp.dot(
                act[pl.ds(section * slot_rows, slot_rows), :],
                w_out[:, columns],
                preferred_element_type=jnp.float32,
            ).astype(jnp.bfloat16)
            ys[j % 3, section] = result.reshape(blocks + (room, wide))
        for copy in first_copies(which, j):
            copy.start()

    def make_weights():
        row = lax.broadcasted_iota(jnp.int32, (room, tok_rows), 0).astype(jnp.float32)
        for which in range(2):

            @pl.loop(0, side)
            def _(q):
                info = told[spread_index(q, plan.leaf[which], mine[plan.leaf[which]])]
                pieces = []
                for k in (0, 1, 2 + 2 * which, 3 + 2 * which):
                    hit = info[k : k + 1, :] == row
                    pieces.append(jnp.where(hit, info[6 + k : 7 + k, :], 0.0))
                pad = -(4 * room) % LANES
                if pad:
                    pieces.append(jnp.zeros((pad, tok_rows), jnp.float32))
                turned = jnp.concatenate(pieces, axis=0).T
                wts[which, q] = turned[:, : 4 * room].astype(jnp.bfloat16)

    def combine(which, j):
        for copy in first_copies(which, j):
            copy.wait()
        own = mine[plan.leaf[which]]
        place = plan.count - 1 - plan.leaf[which]

        @pl.loop(0, side, unroll=4)
        def _(q):
            ix = digits(q, plan.stages)
            full = tuple(ix[:place] + [own] + ix[place:])
            both = jnp.concatenate(
                [
                    ys[(j % 3, 1) + full],
                    swapped[(j,) + tuple(ix)],
                    leaf[(j, 0) + tuple(ix)],
                    leaf[(j, 1) + tuple(ix)],
                ],
                axis=0,
            )
            part = jnp.dot(wts[which, q], both, preferred_element_type=jnp.float32)
            parts[0][(j % 2,) + tuple(ix)] = part.astype(jnp.bfloat16)

        for r in range(2):
            send(which, 0, r, j).start()

    def reduce_stage(t, which, j):
        last = t == stages - 1
        for r in range(2):
            send(which, t, r, j).wait()
            bit = plan.rest[which][r][t]
            place = plan.dims(which, r, t).index(bit)
            left = stages - 1 - t

            def total(ix):
                full = tuple(ix[:place] + [mine[bit]] + ix[place:])
                if t == 0:
                    held = parts[0][(j % 2,) + full + (pl.ds(r * half_rows, half_rows),)]
                else:
                    held = parts[t][(j % 2, r) + full]
                return held.astype(jnp.float32) + arrived[t][(j, r) + tuple(ix)].astype(jnp.float32)

            if last:
                columns = pl.ds(pl.multiple_of(j * wide, wide), wide)
                out[pl.ds(r * half_rows, half_rows), columns] = total([])
            else:

                @pl.loop(0, 1 << left)
                def _(e):
                    ix = digits(e, left)
                    parts[t + 1][(j % 2, r) + tuple(ix)] = total(ix).astype(jnp.bfloat16)

            if not last:
                send(which, t + 1, r, j).start()

    steps = [(0, by_parity(project)), (2, by_parity(combine))]
    for t in range(stages):
        steps.append((3 + t, by_parity(functools.partial(reduce_stage, t))))
    run_stages(chunks, steps, make_weights)


def return_call(plan, room, act, w_out, told):
    tok_rows = told.shape[2]
    wide = 2 * LANES
    side = plan.blocks // 2
    chunk_bytes = 2 * wide * (3 * side * room + sum(side >> t for t in range(1, plan.count)) * tok_rows)
    chunks = w_out.shape[1] // wide
    while chunks % 4 == 0 and chunks * chunk_bytes > VMEM_BUDGET:
        chunks //= 2

    def bf(*shape):
        return pltpu.VMEM(shape, jnp.bfloat16)

    def dma(*shape):
        return pltpu.SemaphoreType.DMA(shape)

    two = (2,)
    scratch = [
        bf(2, side, tok_rows, 4 * room),
        bf(3, 2, *(two * plan.count), room, wide),
        bf(chunks, 2, *(two * plan.stages), room, wide),
        bf(chunks, *(two * plan.stages), room, wide),
        bf(2, *(two * plan.stages), tok_rows, wide),
    ]
    for t in range(1, plan.stages):
        scratch.append(bf(2, 2, *(two * (plan.stages - t)), tok_rows // 2, wide))
    sems = [dma(3, 3), dma(chunks, 3)]
    for t in range(plan.stages):
        scratch.append(bf(chunks, 2, *(two * (plan.stages - 1 - t)), tok_rows // 2, wide))
        sems += [dma(2, 2), dma(chunks, 2)]
    piece = chunks * wide
    call = pl.pallas_call(
        functools.partial(return_kernel, plan, chunks),
        out_shape=jax.ShapeDtypeStruct((tok_rows, piece), jnp.float32),
        in_specs=[pl.BlockSpec(memory_space=pltpu.VMEM)] * 3,
        out_specs=pl.BlockSpec(memory_space=pltpu.VMEM),
        scratch_shapes=scratch + sems,
        compiler_params=pltpu.CompilerParams(
            collective_id=0, has_side_effects=True, vmem_limit_bytes=VMEM_LIMIT
        ),
        name="return_sum",
    )
    pieces = [
        call(act, w_out[:, start : start + piece], told)
        for start in range(0, w_out.shape[1], piece)
    ]
    return pieces[0] if len(pieces) == 1 else jnp.concatenate(pieces, axis=1)


def gather_kernel(plan, chunks, x, info, gains, w_in, act, info_out, *rest):
    (held, info_got, picks, scale, keep, give, got, lhs, hid, w_buf) = rest[:10]
    sems = rest[10:]
    blocks = plan.blocks
    side = blocks // 2
    seg = lax.axis_index("segment")
    me = lax.axis_index("expert")
    mine = [bit_of(me, bit) for bit in range(plan.count)]
    tok_rows, half = x.shape
    half_rows = tok_rows // 2
    wide = half // chunks
    room = keep.shape[-2]
    slot_rows = blocks * room
    units = act.shape[1]

    barrier = pltpu.get_barrier_semaphore()
    friends = [(1 - seg, me)] + [(1 - seg, flip(me, bit)) for bit in plan.leaf]
    for friend in friends:
        pl.semaphore_signal(barrier, inc=1, device_id=friend, device_id_type=MESH)

    @pl.loop(1, blocks)
    def _(k):
        pl.semaphore_signal(
            barrier, inc=1, device_id=(seg, (me + k) % blocks), device_id_type=MESH
        )

    pl.semaphore_wait(barrier, blocks - 1 + len(friends))

    def tell(k):
        to = (me + k) % blocks
        return remote(
            info.at[to], info_got.at[me], sems[0].at[k - 1], sems[1].at[k - 1], (seg, to)
        )

    def columns(j):
        return pl.ds(pl.multiple_of(j * wide, wide), wide)

    def send(which, t, r, j):
        order = plan.rest[which][r]
        bit = order[plan.stages - 1 - t]
        free = order[plan.stages - t :]
        rows = pl.ds(r * half_rows, half_rows)
        index = tuple(slice(None) if d in free else mine[d] for d in plan.dims(which, r, 0))
        dst = held.at[(j,) + index + (rows,)]
        return remote(
            x.at[rows, columns(j)] if t == 0 else dst,
            dst,
            sems[6 + 2 * t].at[j % 2, r],
            sems[7 + 2 * t].at[j, r],
            (seg, flip(me, bit)),
        )

    def first_send(which, j):
        for r in range(2):
            send(which, 0, r, j).start()
        index = tuple(mine[d] for d in plan.dims(which, 0, 0))
        held[(j,) + index] = x[:, columns(j)]

    def relay(t, which, j):
        for r in range(2):
            send(which, t - 1, r, j).wait()
            send(which, t, r, j).start()

    def last_copies(which, j):
        nbr = flip(me, plan.leaf[which])
        peers = ((1 - seg, me), (seg, nbr), (1 - seg, nbr))
        return [
            remote(
                give.at[j % 3, k],
                got.at[j, k],
                sems[2].at[j % 3, k],
                sems[3].at[j, k],
                peer,
            )
            for k, peer in enumerate(peers)
        ]

    def weight_copies(j):
        copies = []
        for which, owner in enumerate((seg, 1 - seg)):
            rows = pl.ds(pl.multiple_of(owner * half + j * wide, wide), wide)
            copies.append(
                pltpu.make_async_copy(
                    w_in.at[rows, :],
                    w_buf.at[j % 3, pl.ds(which * wide, wide)],
                    sems[4].at[j % 3, which],
                )
            )
        return copies

    def read_info():
        info_got[me] = info[me]

        @pl.loop(1, blocks)
        def _(k):
            tell(k).wait()

        row = lax.broadcasted_iota(jnp.int32, (room, tok_rows), 0).astype(jnp.float32)

        @pl.loop(0, blocks)
        def _(d):
            told = info_got[d]
            info_out[d] = told
            own = told[0:1, :] == row
            factor = jnp.sum(
                jnp.where(own, told[FACTOR_ROW : FACTOR_ROW + 1, :], 0.0), axis=1, keepdims=True
            )
            rows = pl.ds(pl.multiple_of(d * room, room), room)
            scale[rows, :] = jnp.broadcast_to(factor, (room, wide))

        for which in range(2):

            @pl.loop(0, side)
            def _(q):
                told = info_got[spread_index(q, plan.leaf[which], mine[plan.leaf[which]])]
                picks[which, q] = jnp.concatenate(
                    [
                        jnp.where(told[k : k + 1, :] == row, 1.0, 0.0)
                        for k in (0, 1, 2 + 2 * which, 3 + 2 * which)
                    ],
                    axis=0,
                ).astype(jnp.bfloat16)

    def pick(which, j):
        for copy in weight_copies(j):
            copy.start()
        for r in range(2):
            send(which, plan.stages - 1, r, j).wait()

        @pl.when(j == 0)
        def _():
            read_info()

        @pl.loop(0, side, unroll=4)
        def _(q):
            there = held[(j,) + tuple(digits(q, plan.stages))]
            taken = jnp.dot(picks[which, q], there, preferred_element_type=jnp.float32)
            taken = taken.astype(jnp.bfloat16)
            keep[j % 3, q] = taken[:room]
            for k in range(3):
                give[j % 3, k, q] = taken[(k + 1) * room : (k + 2) * room]

        for copy in last_copies(which, j):
            copy.start()

    def multiply(which, j):
        for copy in last_copies(which, j):
            copy.wait()
        for copy in weight_copies(j):
            copy.wait()
        bit = plan.leaf[which]
        places = [
            pl.ds(pl.multiple_of(owner * half + j * wide, wide), wide) for owner in (seg, 1 - seg)
        ]
        factors = [[gains[pl.ds(section, 1), place] for place in places] for section in range(2)]

        @pl.loop(0, side, unroll=2)
        def _(q):
            for own, sources in (
                (mine[bit], (keep.at[j % 3, q], got.at[j, 0, q])),
                (1 - mine[bit], (got.at[j, 1, q], got.at[j, 2, q])),
            ):
                base = spread_index(q, bit, own) * room
                factor = scale[pl.ds(pl.multiple_of(base, room), room), :]
                for f, source in enumerate(sources):
                    scaled = source[...].astype(jnp.float32) * factor
                    for section in range(2):
                        to = pl.ds(pl.multiple_of(section * slot_rows + base, room), room)
                        lhs[to, pl.ds(f * wide, wide)] = (scaled * factors[section][f]).astype(
                            jnp.bfloat16
                        )

        for section in range(2):
            rows = pl.ds(section * slot_rows, slot_rows)
            hid[rows, :] += jnp.dot(
                lhs[rows, :], w_buf[j % 3], preferred_element_type=jnp.float32
            )

    tile = math.gcd(slot_rows, 256)

    def clear():
        @pl.loop(0, 2 * slot_rows // tile)
        def _(r):
            rows = pl.ds(pl.multiple_of(r * tile, tile), tile)
            hid[rows, :] = jnp.zeros((tile, 2 * units), jnp.float32)

    @pl.loop(1, blocks)
    def _(k):
        tell(k).start()

    steps = [(0, by_parity(first_send))]
    for t in range(1, plan.stages):
        steps.append((t, by_parity(functools.partial(relay, t))))
    steps += [(plan.stages, by_parity(pick)), (plan.stages + 2, by_parity(multiply))]
    run_stages(chunks, steps, clear)

    @pl.loop(0, 2 * slot_rows // tile)
    def _(r):
        rows = pl.ds(pl.multiple_of(r * tile, tile), tile)
        gate = hid[rows, :units]
        act[rows, :] = (gate / (1.0 + jnp.exp(-gate)) * hid[rows, units:]).astype(jnp.bfloat16)


def gather_call(plan, room, x, info, gains, w_in):
    blocks = plan.blocks
    side = blocks // 2
    tok_rows, half = x.shape
    wide = LANES
    chunks = half // wide
    slot_rows = blocks * room
    units = w_in.shape[1] // 2

    def bf(*shape):
        return pltpu.VMEM(shape, jnp.bfloat16)

    def f32(*shape):
        return pltpu.VMEM(shape, jnp.float32)

    def dma(*shape):
        return pltpu.SemaphoreType.DMA(shape)

    scratch = [
        bf(chunks, *((2,) * plan.stages), tok_rows, wide),
        f32(*info.shape),
        bf(2, side, 4 * room, tok_rows),
        f32(slot_rows, wide),
        bf(3, side, room, wide),
        bf(3, 3, side, room, wide),
        bf(chunks, 3, side, room, wide),
        bf(2 * slot_rows, 2 * wide),
        f32(2 * slot_rows, 2 * units),
        bf(3, 2 * wide, 2 * units),
    ]
    sems = [dma(blocks - 1), dma(blocks - 1), dma(3, 3), dma(chunks, 3), dma(3, 2), dma(1)]
    for _ in range(plan.stages):
        sems += [dma(2, 2), dma(chunks, 2)]
    vmem = pl.BlockSpec(memory_space=pltpu.VMEM)
    return pl.pallas_call(
        functools.partial(gather_kernel, plan, chunks),
        out_shape=(
            jax.ShapeDtypeStruct((2 * slot_rows, units), jnp.bfloat16),
            jax.ShapeDtypeStruct(info.shape, jnp.float32),
        ),
        in_specs=[vmem, vmem, vmem, pl.BlockSpec(memory_space=pl.ANY)],
        out_specs=(vmem, vmem),
        scratch_shapes=scratch + sems,
        compiler_params=pltpu.CompilerParams(
            collective_id=1, has_side_effects=True, vmem_limit_bytes=VMEM_LIMIT
        ),
        name="gather_hidden",
    )(x, info, gains, w_in)


def swap_cores(x):
    count = lax.axis_size("segment")
    return lax.ppermute(x, "segment", [(i, count - 1 - i) for i in range(count)])


def inverse_rms(values):
    return lax.rsqrt(jnp.mean(values * values, axis=-1, keepdims=True) + 1e-06)


def per_device(
    rollout,
    norm_gain,
    router_first,
    gain_second,
    router_second,
    expert_ids,
    copy_pick,
    later_ids,
    slot_table,
    expert_in,
    expert_out,
):
    position = lax.axis_index("segment")
    segment_count = lax.axis_size("segment")
    chip_count = lax.axis_size("expert")
    tok_rows, half = rollout.shape
    top_count = expert_ids.shape[1]
    experts_all = router_first.shape[2]
    slot_count = slot_table.shape[0]
    capacity = 3 * tok_rows * top_count // (2 * segment_count * chip_count)

    expert_cols = jnp.arange(experts_all, dtype=jnp.int32)
    slot_ids = jnp.arange(slot_count, dtype=jnp.int32)
    same = slot_table[:, None] == slot_table[None, :]
    earlier = slot_ids[:, None] < slot_ids[None, :]
    copy_rank = jnp.sum((same & earlier).astype(jnp.int32), axis=0)
    slot_holders = jnp.sum(same.astype(jnp.int32), axis=0)
    here = slot_table == expert_ids[..., None]
    copies = jnp.max(jnp.where(here, slot_holders, 1), axis=-1)
    wanted = copy_pick % copies
    match = here & (copy_rank == wanted[..., None])
    hit = jnp.sum(match.astype(jnp.bfloat16), axis=1)
    order = jnp.arange(tok_rows, dtype=jnp.int32)
    before_mask = (order[None, :] < order[:, None]).astype(jnp.bfloat16)
    before = jnp.dot(before_mask, hit, preferred_element_type=jnp.float32).astype(jnp.int32)
    other_half = swap_cores(rollout)
    first = position == 0
    left = jnp.where(first, rollout, other_half)
    right = jnp.where(first, other_half, rollout)
    whole = jnp.concatenate([left, right], axis=1)
    states_in = whole.astype(jnp.float32)
    factor = inverse_rms(states_in)
    normed = (states_in * factor * norm_gain[0].astype(jnp.float32)).astype(
        jnp.bfloat16
    )
    logits = jnp.dot(normed, router_first[0], preferred_element_type=jnp.float32)
    picked = expert_ids[..., None] == expert_cols
    chosen = jnp.sum(jnp.where(picked, logits[:, None, :], 0.0), axis=-1)
    lifted = jnp.exp(chosen - jnp.max(chosen, axis=1, keepdims=True))
    gates = (lifted / jnp.sum(lifted, axis=1, keepdims=True)).astype(jnp.bfloat16)
    place = jnp.where((hit > 0) & (before < capacity), before, -1).astype(jnp.float32)
    gate = jnp.sum(jnp.where(match, gates.astype(jnp.float32)[..., None], 0.0), axis=1)

    plan = Plan(grid_sides(chip_count))

    def by_core(values):
        cores = values.T.reshape(segment_count, chip_count, tok_rows)
        own = jnp.where(first, cores[0], cores[1])
        other = jnp.where(first, cores[1], cores[0])
        rows = [own, other]
        for bit in plan.leaf:
            for core in (own, other):
                paired = core.reshape(-1, 2, 1 << bit, tok_rows)
                rows.append(paired[:, ::-1].reshape(chip_count, tok_rows))
        return rows

    factors = jnp.broadcast_to(factor[:, 0], (chip_count, tok_rows))
    blank = jnp.zeros((chip_count, tok_rows), jnp.float32)
    info = jnp.stack(by_core(place) + by_core(gate) + [factors, blank, blank, blank], axis=1)
    gains = jnp.concatenate([swap_cores(norm_gain), norm_gain], axis=0).astype(jnp.float32)
    room = -(-capacity // 16) * 16
    active, told = gather_call(plan, room, rollout, info, gains, expert_in[0])
    summed = return_call(plan, room, active, expert_out[0], told)
    mixed = states_in + summed
    later = (mixed * inverse_rms(mixed) * gain_second[0].astype(jnp.float32)).astype(jnp.bfloat16)
    logp = jax.nn.log_softmax(
        jnp.dot(later, router_second[0], preferred_element_type=jnp.float32), axis=-1
    )
    later_pick = later_ids[..., None] == expert_cols
    score = jnp.sum(jnp.where(later_pick, logp[:, None, :], 0.0), axis=(1, 2))
    partner = swap_cores(score)
    ratio = jnp.where(position == 1, score - partner, partner - score)
    paired = ratio.reshape(tok_rows // 2, 2)
    column = lax.dynamic_slice_in_dim(paired, position, 1, 1)
    return (mixed.astype(jnp.bfloat16)[None], column)


def solution(mesh):
    in_specs = (
        P("expert", "segment"),
        P("segment", None),
        P("segment", None, None),
        P("segment", None),
        P("segment", None, None),
        P("expert", None),
        P("expert", None),
        P("expert", None),
        P(),
        P(("segment", "expert"), None, None),
        P(("segment", "expert"), None, None),
    )
    out_specs = (P("segment", "expert", None), P("expert", "segment"))
    return jax.shard_map(
        per_device, mesh=mesh, in_specs=in_specs, out_specs=out_specs, check_vma=False
    )
```

profile of v0, /device:TPU:0, one launch (start us, length us, event | category | flops | bytes accessed | tf_op | source)
XLA Modules:
  0.0 228.5 jit_solution(13849442323250732959)
XLA Ops:
  0.6 0.0 copy-start
  0.7 0.6 collective-permute-start
  1.2 0.1 collective-permute-start.1
  1.3 0.8 convert_reduce_fusion
  2.1 0.8 fusion.12
  2.9 0.8 add_select_fusion
  3.7 0.8 fusion.14
  4.5 0.1 select_convert_fusion
  4.6 0.8 mul.62
  5.4 0.7 mul.63
  6.2 0.0 collective-permute-done.1
  6.2 1.4 maximum_convert_fusion.gains
  7.5 0.0 collective-permute-done
  7.5 1.1 broadcast_select_fusion.1
  8.7 0.0 copy-start.2
  8.7 0.0 copy-start.3
  8.7 0.3 fusion
  9.0 0.5 fusion.4
  9.5 0.0 copy-done.2
  9.6 0.1 select_reduce_fusion
  10.0 1.4 stack.23.info
  11.4 85.2 %gather_hidden.1 = (bf16[1536,768]{1,0:T(8,128)(2,1)}, f32[16,16,128]{2,1,0:T(8,128)}) custom-call(bf16[128,2048]{1,0:T(8,128)(2,1)} %x.1, f32[16,16,128]{2,1,0:T(8,128)} %stack.23.info, f32[2,4096]{1,0:T(2,128)} %maximum_convert_fusion.gains, bf16[4096,1536]{1,0:T(8,128)(2,1)} %bitcast.46), custom_call_target="tpu_custom_call" | custom-call | tf_op jit(solution)/shard_map/gather_hidden/pallas_call | solution.py:542
  96.6 126.1 %return_sum.1 = f32[128,4096]{1,0:T(8,128)} custom-call(bf16[1536,768]{1,0:T(8,128)(2,1)} %get-tuple-element.4.act, bf16[768,4096]{1,0:T(8,128)(2,1)} %bitcast.47, f32[16,16,128]{2,1,0:T(8,128)} %get-tuple-element.5.told), custom_call_target="tpu_custom_call" | custom-call | tf_op jit(solution)/shard_map/return_sum/pallas_call | solution.py:299
  222.7 0.0 copy-start.1
  222.7 3.0 %multiply_reduce_fusion = (f32[128]{0:T(128)S(1)}, bf16[1,128,4096]{2,1,0:T(8,128)(2,1)}) fusion(f32[128,4096]{1,0:T(8,128)} %return_sum.1, bf16[128,2048]{1,0:T(8,128)(2,1)S(1)} %get-tuple-element.17, bf16[128,2048]{1,0:T(8,128)(2,1)S(1)} %get-tuple-element.16), kind=kLoop, calls=%fused_computation.7 | loop fusion | flops 4194176 | bytes 4194816 | tf_op jit(solution)/shard_map/reduce_sum | solution.py:564
  225.8 0.6 fusion.18
  226.4 0.0 copy-done.4
  226.5 0.1 collective-permute-start.2
  226.5 1.1 collective-permute-done.2
  227.7 0.1 reshape.116
  227.8 0.1 constant_dynamic-slice_fusion
  227.9 0.6 copy.36
  (29 shorter events, 0.4 us)
Async XLA Ops:
  0.6 225.1 %copy-start = (bf16[1,4096,28]{1,2,0:T(8,128)(2,1)S(1)}, bf16[1,4096,28]{1,2,0:T(8,128)(2,1)}, u32[]{:S(2)}) copy-start(bf16[1,4096,28]{1,2,0:T(8,128)(2,1)} %param.15) | copy-start | bytes 688132
  0.6 8.3 %copy-start.5 = (bf16[1,4096,28]{1,2,0:T(8,128)(2,1)S(1)}, bf16[1,4096,28]{1,2,0:T(8,128)(2,1)}, u32[]{:S(2)}) copy-start(bf16[1,4096,28]{1,2,0:T(8,128)(2,1)} %param.13) | copy-start | bytes 688132
  0.7 6.9 %collective-permute-start = (bf16[128,2048]{1,0:T(8,128)(2,1)}, bf16[128,2048]{1,0:T(8,128)(2,1)S(1)}, u32[]{:S(2)}, u32[]{:S(2)}) collective-permute-start(bf16[128,2048]{1,0:T(8,128)(2,1)} %x.1), channel_id=1, source_target_pairs={{0,16},{16,0},{1,17},{17,1},{2,18},{18,2},{3,19},{19,3},{4,20},{20... | collective-permute-start | bytes 1572872 | tf_op jit(solution)/shard_map/ppermute | solution.py:560
  1.2 4.9 %collective-permute-start.1 = (bf16[1,4096]{1,0:T(2,128)(2,1)}, bf16[1,4096]{1,0:T(2,128)(2,1)S(1)}, u32[]{:S(2)}, u32[]{:S(2)}) collective-permute-start(bf16[1,4096]{1,0:T(2,128)(2,1)} %param.12), channel_id=1, source_target_pairs={{0,16},{16,0},{1,17},{17,1},{2,18},{18,2},{3,19},{19,3},{4,20},{20... | collective-permute-start | bytes 24584 | tf_op jit(solution)/shard_map/ppermute | solution.py:560
  8.7 0.9 copy-start.2
  8.7 1.0 copy-start.3
  222.7 3.0 %copy-start.1 = (f32[128,4096]{1,0:T(8,128)S(1)}, f32[128,4096]{1,0:T(8,128)}, u32[]{:S(2)}) copy-start(f32[128,4096]{1,0:T(8,128)} %return_sum.1) | copy-start | bytes 6291460
  225.7 0.7 copy-start.4
  226.5 1.2 collective-permute-start.2
where the time goes:
time: 229 us; the launch traced here: 228 us
  Pallas kernels  211 us (92%)
  other arithmetic  10.8 us (5%)
  local copies, waits for them, and re-layouts  2.46 us (1%)
    pallas_call x1, Pallas kernels, return_call(): call(act, w_out[:, start:start + piece], told)  126 us
    pallas_call x1, Pallas kernels, gather_call(): pl.pallas_call(functools.partial(gather_kernel, plan, chunks), out_shape=...  85.2 us
  transfers between devices with their start and end apart: 3, of which 1 were waited for; matrix products, arithmetic and copies ran while one was open for 3% of the time, Pallas kernels for 0%

commit v1 on v0

--- a/solution.py
+++ b/solution.py
@@ -11,9 +11,12 @@
 LANES = 128
 VMEM_BUDGET = 26 << 20
 VMEM_LIMIT = 60 * 1024 * 1024
+VMEM_MOST = 67043328
+VMEM_SPARE = 4 << 20
 MESH = pl.DeviceIdType.MESH
 INFO_ROWS = 16
 FACTOR_ROW = 12
+EPS = 1e-06
 
 
 def grid_sides(count):
@@ -44,6 +47,10 @@
         self.rest = [[order[1:] for order in pair] for pair in orders]
         self.stages = self.count - 1
 
+    def split(self, rows):
+        part = max(3 * rows // 8 // 16 * 16, 16)
+        return part, rows - part
+
     def dims(self, which, order, done):
         used = [self.leaf[which]] + self.rest[which][order][:done]
         return [bit for bit in reversed(range(self.count)) if bit not in used]
@@ -77,7 +84,7 @@
     )
 
 
-def run_stages(chunks, stages, after_first=None):
+def run_stages(chunks, stages, hooks):
     depth = max(lag for lag, _ in stages)
 
     @pl.loop(0, chunks + depth)
@@ -88,11 +95,11 @@
             def _():
                 stage(step - lag)
 
-        if after_first is not None:
-
-            @pl.when(step == 0)
+        for when, hook in hooks.items():
+
+            @pl.when(step == when)
             def _():
-                after_first()
+                hook()
 
 
 def by_parity(stage):
@@ -106,26 +113,92 @@
     return run
 
 
-def return_kernel(plan, chunks, act, w_out, told, out, wts, ys, leaf, swapped, *rest):
+def meet(plan, seg, me, friends, everyone):
+    barrier = pltpu.get_barrier_semaphore()
+    for friend in friends:
+        pl.semaphore_signal(barrier, inc=1, device_id=friend, device_id_type=MESH)
+    if everyone:
+
+        @pl.loop(1, plan.blocks)
+        def _(k):
+            pl.semaphore_signal(
+                barrier, inc=1, device_id=(seg, (me + k) % plan.blocks), device_id_type=MESH
+            )
+
+    pl.semaphore_wait(barrier, len(friends) + (plan.blocks - 1 if everyone else 0))
+
+
+def cross_friends(plan, seg, me):
+    return [(1 - seg, me)] + [(1 - seg, flip(me, bit)) for bit in plan.leaf]
+
+
+def make_weights(plan, seg, me, room, told, wts):
+    tok_rows = told.shape[-1]
+    row = lax.broadcasted_iota(jnp.int32, (room, tok_rows), 0).astype(jnp.float32)
+    for which in range(2):
+        bit = plan.leaf[which]
+
+        @pl.loop(0, plan.blocks // 2)
+        def _(q):
+            info = told[spread_index(q, bit, bit_of(me, bit))]
+            pieces = []
+            for k in (0, 1, 2 + 2 * which, 3 + 2 * which):
+                hit = info[k : k + 1, :] == row
+                pieces.append(jnp.where(hit, info[6 + k : 7 + k, :], 0.0))
+            pad = -(4 * room) % LANES
+            if pad:
+                pieces.append(jnp.zeros((pad, tok_rows), jnp.float32))
+            turned = jnp.concatenate(pieces, axis=0).T
+            wts[which, q] = turned[:, : 4 * room].astype(jnp.bfloat16)
+
+
+def return_scratch(plan, room, tok_rows, chunks):
+    def bf(*shape):
+        return pltpu.VMEM(shape, jnp.bfloat16)
+
+    def dma(*shape):
+        return pltpu.SemaphoreType.DMA(shape)
+
+    side = plan.blocks // 2
+    low = (2,) * plan.stages
+    split = plan.split(tok_rows)
+    scratch = [
+        bf(2, side, tok_rows, 4 * room),
+        bf(2, 2, 2, *((2,) * plan.count), room, LANES),
+        bf(chunks, 2, 2, *low, room, LANES),
+        bf(chunks, 2, *low, room, LANES),
+        bf(2, 2, *low, tok_rows, LANES),
+    ]
+    sems = [dma(2, 2, 3), dma(chunks, 2, 3)]
+    for t in range(plan.stages):
+        for rows in split:
+            left = (2,) * (plan.stages - 1 - t)
+            scratch.append(bf(chunks, 2, *left, rows, LANES))
+            if t + 1 < plan.stages:
+                scratch.append(bf(2, 2, *left, rows, LANES))
+        sems += [dma(2, 2, 2), dma(chunks, 2, 2)]
+    return scratch, sems
+
+
+def return_steps(plan, seg, me, act, w_out, finish, scratch, sems):
+    wts, ys, leaf, swapped, first = scratch[:5]
+    more = list(scratch[5:])
     stages = plan.stages
-    parts, arrived, sems = rest[:stages], rest[stages : 2 * stages], rest[2 * stages :]
-    seg = lax.axis_index("segment")
-    me = lax.axis_index("expert")
+    arrived, parts = [], []
+    for t in range(stages):
+        arrived.append([])
+        parts.append([])
+        for _ in range(2):
+            arrived[t].append(more.pop(0))
+            if t + 1 < stages:
+                parts[t].append(more.pop(0))
     side = plan.blocks // 2
     room = ys.shape[-2]
-    wide = ys.shape[-1]
     slot_rows = plan.blocks * room
-    tok_rows = out.shape[0]
-    half_rows = tok_rows // 2
+    tok_rows = first.shape[-2]
+    split = plan.split(tok_rows)
+    spans = (pl.ds(0, split[0]), pl.ds(split[0], split[1]))
     mine = [bit_of(me, bit) for bit in range(plan.count)]
-
-    barrier = pltpu.get_barrier_semaphore()
-    friends = [(1 - seg, me)]
-    friends += [(seg, flip(me, bit)) for bit in range(plan.count)]
-    friends += [(1 - seg, flip(me, bit)) for bit in plan.leaf]
-    for friend in friends:
-        pl.semaphore_signal(barrier, inc=1, device_id=friend, device_id_type=MESH)
-    pl.semaphore_wait(barrier, len(friends))
 
     def region(which, own):
         bit = plan.leaf[which]
@@ -136,35 +209,37 @@
         )
 
     def first_copies(which, j):
-        slot = j % 3
         nbr = flip(me, plan.leaf[which])
         sources = (
-            (ys.at[(slot, 1) + region(which, False)], leaf.at[j, 0], (seg, nbr)),
-            (ys.at[(slot, 0) + region(which, False)], leaf.at[j, 1], (1 - seg, nbr)),
-            (ys.at[(slot, 0) + region(which, True)], swapped.at[j], (1 - seg, me)),
+            (ys.at[(j % 2, which, 1) + region(which, False)], leaf.at[j, which, 0], (seg, nbr)),
+            (ys.at[(j % 2, which, 0) + region(which, False)], leaf.at[j, which, 1], (1 - seg, nbr)),
+            (ys.at[(j % 2, which, 0) + region(which, True)], swapped.at[j, which], (1 - seg, me)),
         )
         return [
-            remote(src, dst, sems[0].at[slot, k], sems[1].at[j, k], peer)
+            remote(src, dst, sems[0].at[j % 2, which, k], sems[1].at[j, which, k], peer)
             for k, (src, dst, peer) in enumerate(sources)
         ]
+
+    def held_at(which, t, r, j, index):
+        if t == 0:
+            return (j % 2, which) + index + (spans[r],)
+        return (j % 2, which) + index
 
     def send(which, t, r, j):
         bit = plan.rest[which][r][t]
         dims = plan.dims(which, r, t)
         index = tuple(1 - mine[d] if d == bit else slice(None) for d in dims)
-        if t == 0:
-            src = parts[0].at[(j % 2,) + index + (pl.ds(r * half_rows, half_rows),)]
-        else:
-            src = parts[t].at[(j % 2, r) + index]
+        source = first if t == 0 else parts[t - 1][r]
         return remote(
-            src,
-            arrived[t].at[j, r],
-            sems[2 + 2 * t].at[j % 2, r],
-            sems[3 + 2 * t].at[j, r],
+            source.at[held_at(which, t, r, j, index)],
+            arrived[t][r].at[j, which],
+            sems[2 + 2 * t].at[j % 2, which, r],
+            sems[3 + 2 * t].at[j, which, r],
             (seg, flip(me, bit)),
         )
 
-    def project(which, j):
+    def project(j):
+        wide = 2 * LANES
         columns = pl.ds(pl.multiple_of(j * wide, wide), wide)
         blocks = (2,) * plan.count
         for section in range(2):
@@ -173,116 +248,103 @@
                 w_out[:, columns],
                 preferred_element_type=jnp.float32,
             ).astype(jnp.bfloat16)
-            ys[j % 3, section] = result.reshape(blocks + (room, wide))
-        for copy in first_copies(which, j):
-            copy.start()
-
-    def make_weights():
-        row = lax.broadcasted_iota(jnp.int32, (room, tok_rows), 0).astype(jnp.float32)
+            for which in range(2):
+                half = result[:, which * LANES : (which + 1) * LANES]
+                ys[j % 2, which, section] = half.reshape(blocks + (room, LANES))
         for which in range(2):
-
-            @pl.loop(0, side)
+            for copy in first_copies(which, j):
+                copy.start()
+
+    def combine(j):
+        for which in range(2):
+            for copy in first_copies(which, j):
+                copy.wait()
+            own = mine[plan.leaf[which]]
+            place = plan.count - 1 - plan.leaf[which]
+
+            @pl.loop(0, side, unroll=8)
             def _(q):
-                info = told[spread_index(q, plan.leaf[which], mine[plan.leaf[which]])]
-                pieces = []
-                for k in (0, 1, 2 + 2 * which, 3 + 2 * which):
-                    hit = info[k : k + 1, :] == row
-                    pieces.append(jnp.where(hit, info[6 + k : 7 + k, :], 0.0))
-                pad = -(4 * room) % LANES
-                if pad:
-                    pieces.append(jnp.zeros((pad, tok_rows), jnp.float32))
-                turned = jnp.concatenate(pieces, axis=0).T
-                wts[which, q] = turned[:, : 4 * room].astype(jnp.bfloat16)
-
-    def combine(which, j):
-        for copy in first_copies(which, j):
-            copy.wait()
-        own = mine[plan.leaf[which]]
-        place = plan.count - 1 - plan.leaf[which]
-
-        @pl.loop(0, side, unroll=4)
-        def _(q):
-            ix = digits(q, plan.stages)
-            full = tuple(ix[:place] + [own] + ix[place:])
-            both = jnp.concatenate(
-                [
-                    ys[(j % 3, 1) + full],
-                    swapped[(j,) + tuple(ix)],
-                    leaf[(j, 0) + tuple(ix)],
-                    leaf[(j, 1) + tuple(ix)],
-                ],
-                axis=0,
-            )
-            part = jnp.dot(wts[which, q], both, preferred_element_type=jnp.float32)
-            parts[0][(j % 2,) + tuple(ix)] = part.astype(jnp.bfloat16)
-
-        for r in range(2):
-            send(which, 0, r, j).start()
-
-    def reduce_stage(t, which, j):
+                ix = digits(q, stages)
+                full = tuple(ix[:place] + [own] + ix[place:])
+                ix = tuple(ix)
+                both = jnp.concatenate(
+                    [
+                        ys[(j % 2, which, 1) + full],
+                        swapped[(j, which) + ix],
+                        leaf[(j, which, 0) + ix],
+                        leaf[(j, which, 1) + ix],
+                    ],
+                    axis=0,
+                )
+                part = jnp.dot(wts[which, q], both, preferred_element_type=jnp.float32)
+                first[(j % 2, which) + ix] = part.astype(jnp.bfloat16)
+
+            for r in range(2):
+                send(which, 0, r, j).start()
+
+    def reduce_stage(t, j):
         last = t == stages - 1
-        for r in range(2):
-            send(which, t, r, j).wait()
-            bit = plan.rest[which][r][t]
-            place = plan.dims(which, r, t).index(bit)
-            left = stages - 1 - t
-
-            def total(ix):
-                full = tuple(ix[:place] + [mine[bit]] + ix[place:])
-                if t == 0:
-                    held = parts[0][(j % 2,) + full + (pl.ds(r * half_rows, half_rows),)]
+        left = stages - 1 - t
+        for which in range(2):
+            for r in range(2):
+                send(which, t, r, j).wait()
+                bit = plan.rest[which][r][t]
+                place = plan.dims(which, r, t).index(bit)
+                source = first if t == 0 else parts[t - 1][r]
+
+                def total(ix):
+                    full = tuple(ix[:place] + [mine[bit]] + ix[place:])
+                    held = source[held_at(which, t, r, j, full)]
+                    came = arrived[t][r][(j, which) + tuple(ix)]
+                    return held.astype(jnp.float32) + came.astype(jnp.float32)
+
+                if last:
+                    start = pl.multiple_of((2 * j + which) * LANES, LANES)
+                    finish(spans[r], pl.ds(start, LANES), total([]))
                 else:
-                    held = parts[t][(j % 2, r) + full]
-                return held.astype(jnp.float32) + arrived[t][(j, r) + tuple(ix)].astype(jnp.float32)
-
-            if last:
-                columns = pl.ds(pl.multiple_of(j * wide, wide), wide)
-                out[pl.ds(r * half_rows, half_rows), columns] = total([])
-            else:
-
-                @pl.loop(0, 1 << left)
-                def _(e):
-                    ix = digits(e, left)
-                    parts[t + 1][(j % 2, r) + tuple(ix)] = total(ix).astype(jnp.bfloat16)
-
-            if not last:
-                send(which, t + 1, r, j).start()
-
-    steps = [(0, by_parity(project)), (2, by_parity(combine))]
+
+                    @pl.loop(0, 1 << left, unroll=2)
+                    def _(e):
+                        ix = digits(e, left)
+                        parts[t][r][(j % 2, which) + tuple(ix)] = total(ix).astype(jnp.bfloat16)
+
+                    send(which, t + 1, r, j).start()
+
+    steps = [(0, project), (1, combine)]
     for t in range(stages):
-        steps.append((3 + t, by_parity(functools.partial(reduce_stage, t))))
-    run_stages(chunks, steps, make_weights)
+        steps.append((2 + t, functools.partial(reduce_stage, t)))
+    return steps
+
+
+def return_kernel(plan, chunks, act, w_out, told, out, *rest):
+    count = 5 + 4 * plan.stages - 2
+    scratch, sems = rest[:count], rest[count:]
+    seg = lax.axis_index("segment")
+    me = lax.axis_index("expert")
+    friends = cross_friends(plan, seg, me)
+    meet(plan, seg, me, friends + [(seg, flip(me, bit)) for bit in range(plan.count)], False)
+
+    def finish(rows, columns, total):
+        out[rows, columns] = total
+
+    def weights():
+        make_weights(plan, seg, me, scratch[1].shape[-2], told, scratch[0])
+
+    steps = return_steps(plan, seg, me, act, w_out, finish, scratch, sems)
+    run_stages(chunks, steps, {0: weights})
 
 
 def return_call(plan, room, act, w_out, told):
     tok_rows = told.shape[2]
     wide = 2 * LANES
     side = plan.blocks // 2
-    chunk_bytes = 2 * wide * (3 * side * room + sum(side >> t for t in range(1, plan.count)) * tok_rows)
+    chunk_bytes = (
+        2 * wide * (3 * side * room + sum(side >> t for t in range(1, plan.count)) * tok_rows)
+    )
     chunks = w_out.shape[1] // wide
-    while chunks % 4 == 0 and chunks * chunk_bytes > VMEM_BUDGET:
+    while chunks % 2 == 0 and chunks * chunk_bytes > VMEM_BUDGET:
         chunks //= 2
-
-    def bf(*shape):
-        return pltpu.VMEM(shape, jnp.bfloat16)
-
-    def dma(*shape):
-        return pltpu.SemaphoreType.DMA(shape)
-
-    two = (2,)
-    scratch = [
-        bf(2, side, tok_rows, 4 * room),
-        bf(3, 2, *(two * plan.count), room, wide),
-        bf(chunks, 2, *(two * plan.stages), room, wide),
-        bf(chunks, *(two * plan.stages), room, wide),
-        bf(2, *(two * plan.stages), tok_rows, wide),
-    ]
-    for t in range(1, plan.stages):
-        scratch.append(bf(2, 2, *(two * (plan.stages - t)), tok_rows // 2, wide))
-    sems = [dma(3, 3), dma(chunks, 3)]
-    for t in range(plan.stages):
-        scratch.append(bf(chunks, 2, *(two * (plan.stages - 1 - t)), tok_rows // 2, wide))
-        sems += [dma(2, 2), dma(chunks, 2)]
+    scratch, sems = return_scratch(plan, room, tok_rows, chunks)
     piece = chunks * wide
     call = pl.pallas_call(
         functools.partial(return_kernel, plan, chunks),
@@ -302,33 +364,49 @@
     return pieces[0] if len(pieces) == 1 else jnp.concatenate(pieces, axis=1)
 
 
-def gather_kernel(plan, chunks, x, info, gains, w_in, act, info_out, *rest):
-    (held, info_got, picks, scale, keep, give, got, lhs, hid, w_buf) = rest[:10]
-    sems = rest[10:]
+def gather_scratch(plan, room, tok_rows, chunks, units):
+    def bf(*shape):
+        return pltpu.VMEM(shape, jnp.bfloat16)
+
+    def f32(*shape):
+        return pltpu.VMEM(shape, jnp.float32)
+
+    def dma(*shape):
+        return pltpu.SemaphoreType.DMA(shape)
+
     blocks = plan.blocks
     side = blocks // 2
-    seg = lax.axis_index("segment")
-    me = lax.axis_index("expert")
+    slot_rows = blocks * room
+    scratch = [
+        bf(chunks, *((2,) * plan.stages), tok_rows, LANES),
+        f32(blocks, INFO_ROWS, tok_rows),
+        bf(2, side, 4 * room, tok_rows),
+        f32(slot_rows, LANES),
+        bf(3, side, room, LANES),
+        bf(3, 3, side, room, LANES),
+        bf(chunks, 3, side, room, LANES),
+        bf(2 * slot_rows, 2 * LANES),
+        f32(2 * slot_rows, 2 * units),
+        bf(3, 2 * LANES, 2 * units),
+    ]
+    sems = [dma(blocks - 1), dma(blocks - 1), dma(3, 3), dma(chunks, 3), dma(3, 2)]
+    for _ in range(plan.stages):
+        sems += [dma(chunks, 2), dma(chunks, 2)]
+    return scratch, sems
+
+
+def gather_steps(plan, seg, me, x, info, gains, w_in, act, info_out, scratch, sems):
+    (held, info_got, picks, scale, keep, give, got, lhs, hid, w_buf) = scratch
+    blocks = plan.blocks
+    side = blocks // 2
     mine = [bit_of(me, bit) for bit in range(plan.count)]
     tok_rows, half = x.shape
     half_rows = tok_rows // 2
-    wide = half // chunks
+    wide = LANES
     room = keep.shape[-2]
     slot_rows = blocks * room
     units = act.shape[1]
-
-    barrier = pltpu.get_barrier_semaphore()
-    friends = [(1 - seg, me)] + [(1 - seg, flip(me, bit)) for bit in plan.leaf]
-    for friend in friends:
-        pl.semaphore_signal(barrier, inc=1, device_id=friend, device_id_type=MESH)
-
-    @pl.loop(1, blocks)
-    def _(k):
-        pl.semaphore_signal(
-            barrier, inc=1, device_id=(seg, (me + k) % blocks), device_id_type=MESH
-        )
-
-    pl.semaphore_wait(barrier, blocks - 1 + len(friends))
+    tile = math.gcd(slot_rows, 256)
 
     def tell(k):
         to = (me + k) % blocks
@@ -349,8 +427,8 @@
         return remote(
             x.at[rows, columns(j)] if t == 0 else dst,
             dst,
-            sems[6 + 2 * t].at[j % 2, r],
-            sems[7 + 2 * t].at[j, r],
+            sems[5 + 2 * t].at[j, r],
+            sems[6 + 2 * t].at[j, r],
             (seg, flip(me, bit)),
         )
 
@@ -392,6 +470,11 @@
             )
         return copies
 
+    def tell_all():
+        @pl.loop(1, blocks)
+        def _(k):
+            tell(k).start()
+
     def read_info():
         info_got[me] = info[me]
 
@@ -404,7 +487,8 @@
         @pl.loop(0, blocks)
         def _(d):
             told = info_got[d]
-            info_out[d] = told
+            if info_out is not None:
+                info_out[d] = told
             own = told[0:1, :] == row
             factor = jnp.sum(
                 jnp.where(own, told[FACTOR_ROW : FACTOR_ROW + 1, :], 0.0), axis=1, keepdims=True
@@ -480,64 +564,45 @@
                 lhs[rows, :], w_buf[j % 3], preferred_element_type=jnp.float32
             )
 
-    tile = math.gcd(slot_rows, 256)
-
     def clear():
         @pl.loop(0, 2 * slot_rows // tile)
         def _(r):
             rows = pl.ds(pl.multiple_of(r * tile, tile), tile)
             hid[rows, :] = jnp.zeros((tile, 2 * units), jnp.float32)
 
-    @pl.loop(1, blocks)
-    def _(k):
-        tell(k).start()
+    def activate():
+        @pl.loop(0, 2 * slot_rows // tile)
+        def _(r):
+            rows = pl.ds(pl.multiple_of(r * tile, tile), tile)
+            gate = hid[rows, :units]
+            act[rows, :] = (gate / (1.0 + jnp.exp(-gate)) * hid[rows, units:]).astype(jnp.bfloat16)
 
     steps = [(0, by_parity(first_send))]
     for t in range(1, plan.stages):
         steps.append((t, by_parity(functools.partial(relay, t))))
     steps += [(plan.stages, by_parity(pick)), (plan.stages + 2, by_parity(multiply))]
-    run_stages(chunks, steps, clear)
-
-    @pl.loop(0, 2 * slot_rows // tile)
-    def _(r):
-        rows = pl.ds(pl.multiple_of(r * tile, tile), tile)
-        gate = hid[rows, :units]
-        act[rows, :] = (gate / (1.0 + jnp.exp(-gate)) * hid[rows, units:]).astype(jnp.bfloat16)
+    return steps, tell_all, clear, activate
+
+
+def gather_kernel(plan, chunks, x, info, gains, w_in, act, info_out, *rest):
+    scratch, sems = rest[:10], rest[10:]
+    seg = lax.axis_index("segment")
+    me = lax.axis_index("expert")
+    meet(plan, seg, me, cross_friends(plan, seg, me), True)
+    steps, tell_all, clear, activate = gather_steps(
+        plan, seg, me, x, info, gains, w_in, act, info_out, scratch, sems
+    )
+    tell_all()
+    run_stages(chunks, steps, {0: clear})
+    activate()
 
 
 def gather_call(plan, room, x, info, gains, w_in):
-    blocks = plan.blocks
-    side = blocks // 2
     tok_rows, half = x.shape
-    wide = LANES
-    chunks = half // wide
-    slot_rows = blocks * room
+    chunks = half // LANES
+    slot_rows = plan.blocks * room
     units = w_in.shape[1] // 2
-
-    def bf(*shape):
-        return pltpu.VMEM(shape, jnp.bfloat16)
-
-    def f32(*shape):
-        return pltpu.VMEM(shape, jnp.float32)
-
-    def dma(*shape):
-        return pltpu.SemaphoreType.DMA(shape)
-
-    scratch = [
-        bf(chunks, *((2,) * plan.stages), tok_rows, wide),
-        f32(*info.shape),
-        bf(2, side, 4 * room, tok_rows),
-        f32(slot_rows, wide),
-        bf(3, side, room, wide),
-        bf(3, 3, side, room, wide),
-        bf(chunks, 3, side, room, wide),
-        bf(2 * slot_rows, 2 * wide),
-        f32(2 * slot_rows, 2 * units),
-        bf(3, 2 * wide, 2 * units),
-    ]
-    sems = [dma(blocks - 1), dma(blocks - 1), dma(3, 3), dma(chunks, 3), dma(3, 2), dma(1)]
-    for _ in range(plan.stages):
-        sems += [dma(2, 2), dma(chunks, 2)]
+    scratch, sems = gather_scratch(plan, room, tok_rows, chunks, units)
     vmem = pl.BlockSpec(memory_space=pltpu.VMEM)
     return pl.pallas_call(
         functools.partial(gather_kernel, plan, chunks),
@@ -553,6 +618,230 @@
         ),
         name="gather_hidden",
     )(x, info, gains, w_in)
+
+
+def column_sum(values):
+    return jnp.sum(values, axis=1, keepdims=True)
+
+
+def fused_kernel(plan, room, capacity, sizes, *refs):
+    (x, gain, router, gain2, router2, ids, copies, later_ids, table, w_in, w_out) = refs[:11]
+    states, ratio = refs[11:13]
+    n_gather, n_return, n_gather_sems = sizes
+    own = refs[13:25]
+    (whole, gain_got, gains, slots, info, act, w_out_v, mixed, squares, normed, score, score_got) = own
+    gather_refs = refs[25 : 25 + n_gather]
+    return_refs = refs[25 + n_gather : 25 + n_gather + n_return]
+    sems = refs[25 + n_gather + n_return :]
+    swap_sems, sems = sems[:2], sems[2:]
+    gather_sems, return_sems = sems[:n_gather_sems], sems[n_gather_sems:]
+    seg = lax.axis_index("segment")
+    me = lax.axis_index("expert")
+    blocks = plan.blocks
+    tok_rows, half = x.shape
+    full = 2 * half
+    top = ids.shape[0]
+    tiles = full // LANES
+    f32 = jnp.float32
+    partner = (1 - seg, me)
+
+    def tile_at(i):
+        return pl.ds(pl.multiple_of(i * LANES, LANES), LANES)
+
+    own_columns = pl.ds(pl.multiple_of(seg * half, half), half)
+    swap_x = remote(x, whole.at[:, own_columns], swap_sems[0].at[0], swap_sems[1].at[0], partner)
+    swap_gain = remote(gain, gain_got, swap_sems[0].at[1], swap_sems[1].at[1], partner)
+    swap_score = remote(score, score_got, swap_sems[0].at[2], swap_sems[1].at[2], partner)
+    load_w_out = pltpu.make_async_copy(w_out, w_out_v, swap_sems[0].at[3])
+
+    meet(plan, seg, me, cross_friends(plan, seg, me), True)
+    swap_x.start()
+    swap_gain.start()
+    load_w_out.start()
+    steps, tell_all, clear, activate = gather_steps(
+        plan, seg, me, x, info, gains, w_in, act, None, gather_refs, gather_sems
+    )
+
+    def normalize():
+        total = jnp.zeros((tok_rows, LANES), f32)
+        for i in range(tiles):
+            part = whole[:, i * LANES : (i + 1) * LANES].astype(f32)
+            total += part * part
+        return lax.rsqrt(column_sum(total) / full + EPS)
+
+    def prologue():
+        whole[:, own_columns] = x[...]
+        gains[1:2, :] = gain[...].astype(f32)
+        swap_gain.wait()
+        gains[0:1, :] = gain_got[...].astype(f32)
+        swap_x.wait()
+        factor = jnp.broadcast_to(normalize(), (tok_rows, LANES))
+        squares[...] = factor
+
+        @pl.loop(0, tiles)
+        def _(i):
+            part = whole[:, tile_at(i)].astype(f32) * squares[...]
+            normed[:, tile_at(i)] = (part * gains[1:2, tile_at(i)]).astype(jnp.bfloat16)
+
+    def route():
+        slot_count = table.shape[1]
+        line = table[...].astype(f32)
+        i_row = lax.broadcasted_iota(jnp.int32, (slot_count, slot_count), 0)
+        i_col = lax.broadcasted_iota(jnp.int32, (slot_count, slot_count), 1)
+        column = column_sum(jnp.where(i_row == i_col, line, 0.0))
+        same = column == line
+        rank = column_sum(jnp.where(same & (i_col < i_row), 1.0, 0.0))
+        holders = column_sum(jnp.where(same, 1.0, 0.0))
+        wanted = ids[...].astype(f32)
+        choice = copies[...].astype(f32)
+        of_two = choice - 2.0 * jnp.floor(choice * 0.5)
+        of_three = choice - 3.0 * jnp.floor((choice + 0.5) * (1.0 / 3.0))
+        logits = lax.dot_general(
+            router[...], normed[...], (((1,), (1,)), ((), ())), preferred_element_type=f32
+        )
+        names = lax.broadcasted_iota(jnp.int32, logits.shape, 0).astype(f32)
+        matches, chosen = [], []
+        for k in range(top):
+            turn = jnp.where(
+                holders == 1.0,
+                0.0,
+                jnp.where(holders == 2.0, of_two[k : k + 1, :], of_three[k : k + 1, :]),
+            )
+            matches.append((column == wanted[k : k + 1, :]) & (rank == turn))
+            chosen.append(
+                jnp.sum(
+                    jnp.where(names == wanted[k : k + 1, :], logits, 0.0), axis=0, keepdims=True
+                )
+            )
+        most = functools.reduce(jnp.maximum, chosen)
+        lifted = [jnp.exp(value - most) for value in chosen]
+        weight = functools.reduce(jnp.add, lifted)
+        hit = jnp.zeros((slot_count, tok_rows), f32)
+        gate = jnp.zeros((slot_count, tok_rows), f32)
+        for k in range(top):
+            rounded = (lifted[k] / weight).astype(jnp.bfloat16).astype(f32)
+            hit += jnp.where(matches[k], 1.0, 0.0)
+            gate += jnp.where(matches[k], rounded, 0.0)
+        t_row = lax.broadcasted_iota(jnp.int32, (tok_rows, tok_rows), 0)
+        t_col = lax.broadcasted_iota(jnp.int32, (tok_rows, tok_rows), 1)
+        earlier = jnp.where(t_row < t_col, 1.0, 0.0).astype(jnp.bfloat16)
+        before = jnp.dot(hit.astype(jnp.bfloat16), earlier, preferred_element_type=f32)
+        slots[0] = jnp.where((hit > 0.0) & (before < capacity), before, -1.0)
+        slots[1] = gate
+        factor_row = squares[...].T[0:1, :]
+
+        @pl.loop(0, blocks)
+        def _(c):
+            chips = (c, flip(c, plan.leaf[0]), flip(c, plan.leaf[1]))
+            for kind in range(2):
+                for n, chip in enumerate(chips):
+                    for core, which in enumerate((seg, 1 - seg)):
+                        info[c, 6 * kind + 2 * n + core, :] = slots[kind, which * blocks + chip, :]
+            info[c, FACTOR_ROW : FACTOR_ROW + 1, :] = factor_row
+            info[c, FACTOR_ROW + 1 :, :] = jnp.zeros((INFO_ROWS - FACTOR_ROW - 1, tok_rows), f32)
+
+        tell_all()
+
+    def weights():
+        make_weights(plan, seg, me, room, gather_refs[1], return_refs[0])
+
+    chunks = half // LANES
+    run_stages(chunks, steps, {0: prologue, 1: route, 2: clear, plan.stages + 4: weights})
+    activate()
+    load_w_out.wait()
+    squares[...] = jnp.zeros((tok_rows, LANES), f32)
+
+    def finish(rows, columns, total):
+        value = whole[rows, columns].astype(f32) + total
+        mixed[rows, columns] = value
+        states[rows, columns] = value.astype(jnp.bfloat16)
+        squares[rows, :] += value * value
+
+    steps = return_steps(plan, seg, me, act, w_out_v, finish, return_refs, return_sems)
+    run_stages(full // (2 * LANES), steps, {})
+    inverse = lax.rsqrt(column_sum(squares[...]) / full + EPS)
+    squares[...] = jnp.broadcast_to(inverse, (tok_rows, LANES))
+
+    @pl.loop(0, tiles)
+    def _(i):
+        part = mixed[:, tile_at(i)] * squares[...]
+        normed[:, tile_at(i)] = (part * gain2[:, tile_at(i)].astype(f32)).astype(jnp.bfloat16)
+
+    logits = lax.dot_general(
+        router2[...], normed[...], (((1,), (1,)), ((), ())), preferred_element_type=f32
+    )
+    shifted = logits - jnp.max(logits, axis=0, keepdims=True)
+    logp = shifted - jnp.log(jnp.sum(jnp.exp(shifted), axis=0, keepdims=True))
+    names = lax.broadcasted_iota(jnp.int32, logits.shape, 0).astype(f32)
+    wanted = later_ids[...].astype(f32)
+    total = jnp.zeros((1, tok_rows), f32)
+    for k in range(top):
+        total += jnp.sum(jnp.where(names == wanted[k : k + 1, :], logp, 0.0), axis=0, keepdims=True)
+    score[...] = jnp.broadcast_to(total, score.shape)
+    swap_score.start()
+    swap_score.wait()
+    sign = (2 * seg - 1).astype(f32)
+    difference = (score[0:1, :] - score_got[0:1, :]) * sign
+    turned = jnp.broadcast_to(difference, (tok_rows, tok_rows)).T
+    t_row = lax.broadcasted_iota(jnp.int32, (tok_rows, tok_rows), 0)
+    t_col = lax.broadcasted_iota(jnp.int32, (tok_rows, tok_rows), 1)
+    picked = jnp.sum(jnp.where(t_row == 2 * t_col + seg, turned, 0.0), axis=0, keepdims=True)
+    ratio[...] = picked[:, : tok_rows // 2]
+
+
+def fused_scratch(plan, room, tok_rows, half, slot_count, units):
+    chunks = half // LANES
+    full = 2 * half
+    rows = 2 * plan.blocks * room
+    own = [
+        pltpu.VMEM((tok_rows, full), jnp.bfloat16),
+        pltpu.VMEM((1, full), jnp.bfloat16),
+        pltpu.VMEM((2, full), jnp.float32),
+        pltpu.VMEM((2, slot_count, tok_rows), jnp.float32),
+        pltpu.VMEM((plan.blocks, INFO_ROWS, tok_rows), jnp.float32),
+        pltpu.VMEM((rows, units), jnp.bfloat16),
+        pltpu.VMEM((units, full), jnp.bfloat16),
+        pltpu.VMEM((tok_rows, full), jnp.float32),
+        pltpu.VMEM((tok_rows, LANES), jnp.float32),
+        pltpu.VMEM((tok_rows, full), jnp.bfloat16),
+        pltpu.VMEM((8, tok_rows), jnp.float32),
+        pltpu.VMEM((8, tok_rows), jnp.float32),
+    ]
+    gather, gather_sems = gather_scratch(plan, room, tok_rows, chunks, units)
+    back, back_sems = return_scratch(plan, room, tok_rows, full // (2 * LANES))
+    swap = [pltpu.SemaphoreType.DMA((4,)), pltpu.SemaphoreType.DMA((3,))]
+    sizes = (len(gather), len(back), len(gather_sems))
+    return own + gather + back, swap + gather_sems + back_sems, sizes
+
+
+def held_bytes(scratch):
+    total = 0
+    for ref in scratch:
+        *outer, rows, lanes = ref.shape
+        size = jnp.dtype(ref.dtype).itemsize
+        pack = 32 // size
+        total += math.prod(outer) * -(-rows // pack) * pack * -(-lanes // LANES) * LANES * size
+    return total
+
+
+def fused_call(plan, room, capacity, scratch, sems, sizes, *args):
+    tok_rows, half = args[0].shape
+    vmem = pl.BlockSpec(memory_space=pltpu.VMEM)
+    anywhere = pl.BlockSpec(memory_space=pl.ANY)
+    return pl.pallas_call(
+        functools.partial(fused_kernel, plan, room, capacity, sizes),
+        out_shape=(
+            jax.ShapeDtypeStruct((tok_rows, 2 * half), jnp.bfloat16),
+            jax.ShapeDtypeStruct((1, tok_rows // 2), jnp.float32),
+        ),
+        in_specs=[vmem] * 9 + [anywhere] * 2,
+        out_specs=(vmem, vmem),
+        scratch_shapes=scratch + sems,
+        compiler_params=pltpu.CompilerParams(
+            collective_id=2, has_side_effects=True, vmem_limit_bytes=VMEM_MOST
+        ),
+        name="fused_layer",
+    )(*args)
 
 
 def swap_cores(x):
@@ -585,6 +874,32 @@
     experts_all = router_first.shape[2]
     slot_count = slot_table.shape[0]
     capacity = 3 * tok_rows * top_count // (2 * segment_count * chip_count)
+
+    plan = Plan(grid_sides(chip_count))
+    room = -(-capacity // 16) * 16
+    units = expert_out.shape[1]
+    scratch, sems, sizes = fused_scratch(plan, room, tok_rows, half, slot_count, units)
+    if held_bytes(scratch) + VMEM_SPARE < VMEM_MOST:
+        states, column = fused_call(
+            plan,
+            room,
+            capacity,
+            scratch,
+            sems,
+            sizes,
+            rollout,
+            norm_gain,
+            router_first[0].T,
+            gain_second,
+            router_second[0].T,
+            expert_ids.T,
+            copy_pick.T,
+            later_ids.T,
+            slot_table[None, :],
+            expert_in[0],
+            expert_out[0],
+        )
+        return states[None], column.reshape(-1, 1)
 
     expert_cols = jnp.arange(experts_all, dtype=jnp.int32)
     slot_ids = jnp.arange(slot_count, dtype=jnp.int32)
@@ -618,8 +933,6 @@
     place = jnp.where((hit > 0) & (before < capacity), before, -1).astype(jnp.float32)
     gate = jnp.sum(jnp.where(match, gates.astype(jnp.float32)[..., None], 0.0), axis=1)
 
-    plan = Plan(grid_sides(chip_count))
-
     def by_core(values):
         cores = values.T.reshape(segment_count, chip_count, tok_rows)
         own = jnp.where(first, cores[0], cores[1])
@@ -635,7 +948,6 @@
     blank = jnp.zeros((chip_count, tok_rows), jnp.float32)
     info = jnp.stack(by_core(place) + by_core(gate) + [factors, blank, blank, blank], axis=1)
     gains = jnp.concatenate([swap_cores(norm_gain), norm_gain], axis=0).astype(jnp.float32)
-    room = -(-capacity // 16) * 16
     active, told = gather_call(plan, room, rollout, info, gains, expert_in[0])
     summed = return_call(plan, room, active, expert_out[0], told)
     mixed = states_in + summed

time: 229 us -> 209 us (0.913)
  other arithmetic: 10.8 us -> 0 us
  Pallas kernels: 211 us -> 205 us
    pallas_call x2 -> x1, Pallas kernels: 211 us -> 205 us  [fused_call(): pl.pallas_call(functools.partial(fused_kernel, plan, room, capacity, size...]
    reduce_sum x9 -> x0, other arithmetic: 5.16 us -> none  [the longest x2 3.31 us: inverse_rms(): return lax.rsqrt(jnp.mean(values * values, axis=-1, keepdims=True) + 1e-06)]
    unnamed x13 -> x2, local copies, waits for them, and re-layouts: 0.65 us -> 3.4 us
  transfers between devices with their start and end apart: 3 -> 0, of which waited for: 1 -> 0; matrix products, arithmetic and copies ran while one was open for 3% -> 0% of each run, Pallas kernels for 0% -> 0%
where the time goes in v1:
time: 209 us
  Pallas kernels  205 us (98%)
  local copies, waits for them, and re-layouts  3.4 us (2%)
    pallas_call x1, Pallas kernels, fused_call(): pl.pallas_call(functools.partial(fused_kernel, plan, room, capacity, size...  205 us

profile of v1, /device:TPU:0, one launch (start us, length us, event | category | flops | bytes accessed | tf_op | source)
XLA Modules:
  0.0 209.3 jit_solution(9785768999813482344)
XLA Ops:
  0.6 205.3 %fused_layer.1 = (bf16[128,4096]{1,0:T(8,128)(2,1)}, f32[1,64]{1,0:T(1,128)}) custom-call(bf16[128,2048]{1,0:T(8,128)(2,1)} %refs_0_.1, bf16[1,4096]{1,0:T(2,128)(2,1)} %refs_1_.1, bf16[28,4096]{1,0:T(8,128)(2,1)} %bitcast.17, bf16[1,4096]{1,0:T(2,128)(2,1)} %refs_3_.1, bf16[28,4096]{1,0:T(8,128)(2,1)} %bitcast.18, s32[8,128]{1,0:T(8,128)} %bitcast.19, ...), custom_call_target="tpu_custom_call" | custom-call | tf_op jit(solution)/shard_map/fused_layer/pallas_call | solution.py:831
  205.9 2.3 %copy.15 = bf16[1,128,4096]{2,1,0:T(8,128)(2,1)} copy(bf16[1,128,4096]{2,1,0:T(8,128)(2,1)} %bitcast.16) | data formatting | bytes 2097152
  208.2 1.1 copy.16

commit v2 on v1

v2 whole, which is shorter than its diff:
```python
import functools
import math

import jax
import jax.numpy as jnp
from jax import lax
from jax.experimental import pallas as pl
from jax.experimental.pallas import tpu as pltpu
from jax.sharding import PartitionSpec as P

LANES = 128
VMEM_MOST = 67043328
MESH = pl.DeviceIdType.MESH
EPS = 1e-06
RING = 4
LONG_RING = 8
EXTRA_ROWS = 16
NEAR_SLOTS = 6
FACTOR_ROW = 6


def grid_sides(count):
    outer = 1
    while outer**3 < count:
        outer *= 2
    rest = count // outer
    middle = 1
    while middle**2 < rest:
        middle *= 2
    return outer, middle, rest // middle


class Plan:
    def __init__(self, sides):
        logs = [side.bit_length() - 1 for side in sides]
        n_a, n_b, n_c = logs
        bits_c = list(range(n_c))
        bits_b = list(range(n_c, n_c + n_b))
        bits_a = list(range(n_c + n_b, n_c + n_b + n_a))
        self.count = n_a + n_b + n_c
        self.blocks = 1 << self.count
        self.leaf = (bits_c[0], bits_b[0])
        orders = (
            (bits_c + bits_a + bits_b, bits_c + bits_b + bits_a),
            (bits_b + bits_a + bits_c, bits_b + bits_c + bits_a),
        )
        self.rest = [[order[1:] for order in pair] for pair in orders]
        self.stages = self.count - 1

    def split(self, rows):
        part = max(3 * rows // 8 // 16 * 16, 16)
        return part, rows - part

    def dims(self, which, order, done):
        used = [self.leaf[which]] + self.rest[which][order][:done]
        return [bit for bit in reversed(range(self.count)) if bit not in used]


def bit_of(index, bit):
    return (index // (1 << bit)) % 2


def flip(index, bit):
    return index + (1 << bit) * (1 - 2 * bit_of(index, bit))


def digits(value, count):
    return [(value // (1 << (count - 1 - i))) % 2 for i in range(count)]


def spread_index(value, bit, own):
    low = 1 << bit
    return (value // low) * (2 * low) + own * low + value % low


def remote(src, dst, send, recv, peer):
    return pltpu.make_async_remote_copy(
        src_ref=src,
        dst_ref=dst,
        send_sem=send,
        recv_sem=recv,
        device_id=peer,
        device_id_type=MESH,
    )


def run_stages(chunks, stages, early, late):
    depth = max(lag for lag, _ in stages)

    @pl.loop(0, chunks + depth)
    def _(step):
        for lag, stage in stages:
            if lag in early:

                @pl.when(step == lag)
                def _():
                    early[lag]()

            @pl.when((step >= lag) & (step - lag < chunks))
            def _():
                stage(step - lag)

        for when, hook in late.items():

            @pl.when(step == when)
            def _():
                hook()


def by_parity(stage):
    def run(j):
        for which in range(2):

            @pl.when(j % 2 == which)
            def _():
                stage(which, j)

    return run


def near_friends(plan, seg, me):
    friends = [(1 - seg, me)] + [(seg, flip(me, bit)) for bit in range(plan.count)]
    return friends + [(1 - seg, flip(me, bit)) for bit in plan.leaf]


def slots_of(plan, seg, me):
    chips = [me] + [flip(me, bit) for bit in plan.leaf]
    return [core * plan.blocks + chip for chip in chips for core in (seg, 1 - seg)]


def rows_of(which):
    return (0, 1, 2 + 2 * which, 3 + 2 * which)


def make_weights(plan, me, room, places, gates, wts):
    tok_rows = places.shape[-1]
    row = lax.broadcasted_iota(jnp.int32, (room, tok_rows), 0).astype(jnp.float32)
    for which in range(2):
        bit = plan.leaf[which]

        @pl.loop(0, plan.blocks // 2)
        def _(q):
            d = spread_index(q, bit, bit_of(me, bit))
            place, gate = places[d], gates[d]
            pieces = []
            for k in rows_of(which):
                hit = place[k : k + 1, :] == row
                pieces.append(jnp.where(hit, gate[k : k + 1, :], 0.0))
            pad = -(4 * room) % LANES
            if pad:
                pieces.append(jnp.zeros((pad, tok_rows), jnp.float32))
            turned = jnp.concatenate(pieces, axis=0).T
            wts[which, q] = turned[:, : 4 * room].astype(jnp.bfloat16)


def return_scratch(plan, room, tok_rows):
    def bf(*shape):
        return pltpu.VMEM(shape, jnp.bfloat16)

    def dma(*shape):
        return pltpu.SemaphoreType.DMA(shape)

    side = plan.blocks // 2
    low = (2,) * plan.stages
    split = plan.split(tok_rows)
    landing = [
        bf(2, side, tok_rows, 4 * room),
        bf(RING, 2, 2, *low, room, LANES),
        bf(RING, 2, *low, room, LANES),
    ]
    local = [
        bf(2, 2, 2, *((2,) * plan.count), room, LANES),
        bf(2, 2, *low, tok_rows, LANES),
    ]
    sems = [dma(2, 2, 3), dma(RING, 2, 3)]
    for t in range(plan.stages):
        for rows in split:
            left = (2,) * (plan.stages - 1 - t)
            landing.append(bf(RING, 2, *left, rows, LANES))
            if t + 1 < plan.stages:
                local.append(bf(2, 2, *left, rows, LANES))
        sems += [dma(2, 2, 2), dma(RING, 2, 2)]
    return landing, local, sems


def return_steps(plan, seg, me, act, weight_of, finish, landing, local, sems):
    wts, leaf, swapped = landing[:3]
    ys, first = local[:2]
    stages = plan.stages
    arrived = [landing[3 + 2 * t : 5 + 2 * t] for t in range(stages)]
    parts = [local[2 + 2 * t : 4 + 2 * t] for t in range(stages - 1)]
    side = plan.blocks // 2
    room = ys.shape[-2]
    slot_rows = plan.blocks * room
    tok_rows = first.shape[-2]
    split = plan.split(tok_rows)
    spans = (pl.ds(0, split[0]), pl.ds(split[0], split[1]))
    mine = [bit_of(me, bit) for bit in range(plan.count)]

    def region(which, own):
        bit = plan.leaf[which]
        place = plan.count - 1 - bit
        return tuple(
            (mine[bit] if own else 1 - mine[bit]) if i == place else slice(None)
            for i in range(plan.count)
        )

    def first_copies(which, j):
        nbr = flip(me, plan.leaf[which])
        sources = (
            (ys.at[(j % 2, which, 1) + region(which, False)], leaf.at[j % RING, which, 0], (seg, nbr)),
            (ys.at[(j % 2, which, 0) + region(which, False)], leaf.at[j % RING, which, 1], (1 - seg, nbr)),
            (ys.at[(j % 2, which, 0) + region(which, True)], swapped.at[j % RING, which], (1 - seg, me)),
        )
        return [
            remote(src, dst, sems[0].at[j % 2, which, k], sems[1].at[j % RING, which, k], peer)
            for k, (src, dst, peer) in enumerate(sources)
        ]

    def held_at(which, t, r, j, index):
        if t == 0:
            return (j % 2, which) + index + (spans[r],)
        return (j % 2, which) + index

    def send(which, t, r, j):
        bit = plan.rest[which][r][t]
        dims = plan.dims(which, r, t)
        index = tuple(1 - mine[d] if d == bit else slice(None) for d in dims)
        source = first if t == 0 else parts[t - 1][r]
        return remote(
            source.at[held_at(which, t, r, j, index)],
            arrived[t][r].at[j % RING, which],
            sems[2 + 2 * t].at[j % 2, which, r],
            sems[3 + 2 * t].at[j % RING, which, r],
            (seg, flip(me, bit)),
        )

    def project(j):
        weight = weight_of(j)
        blocks = (2,) * plan.count
        for section in range(2):
            result = jnp.dot(
                act[pl.ds(section * slot_rows, slot_rows), :],
                weight[...],
                preferred_element_type=jnp.float32,
            ).astype(jnp.bfloat16)
            for which in range(2):
                half = result[:, which * LANES : (which + 1) * LANES]
                ys[j % 2, which, section] = half.reshape(blocks + (room, LANES))
        for which in range(2):
            for copy in first_copies(which, j):
                copy.start()

    def combine(j):
        for which in range(2):
            for copy in first_copies(which, j):
                copy.wait()
            own = mine[plan.leaf[which]]
            place = plan.count - 1 - plan.leaf[which]

            @pl.loop(0, side, unroll=8)
            def _(q):
                ix = digits(q, stages)
                full = tuple(ix[:place] + [own] + ix[place:])
                ix = tuple(ix)
                both = jnp.concatenate(
                    [
                        ys[(j % 2, which, 1) + full],
                        swapped[(j % RING, which) + ix],
                        leaf[(j % RING, which, 0) + ix],
                        leaf[(j % RING, which, 1) + ix],
                    ],
                    axis=0,
                )
                part = jnp.dot(wts[which, q], both, preferred_element_type=jnp.float32)
                first[(j % 2, which) + ix] = part.astype(jnp.bfloat16)

            for r in range(2):
                send(which, 0, r, j).start()

    def reduce_stage(t, j):
        last = t == stages - 1
        left = stages - 1 - t
        for which in range(2):
            for r in range(2):
                send(which, t, r, j).wait()
                bit = plan.rest[which][r][t]
                place = plan.dims(which, r, t).index(bit)
                source = first if t == 0 else parts[t - 1][r]

                def total(ix):
                    full = tuple(ix[:place] + [mine[bit]] + ix[place:])
                    held = source[held_at(which, t, r, j, full)]
                    came = arrived[t][r][(j % RING, which) + tuple(ix)]
                    return held.astype(jnp.float32) + came.astype(jnp.float32)

                if last:
                    start = pl.multiple_of((2 * j + which) * LANES, LANES)
                    finish(spans[r], pl.ds(start, LANES), total([]))
                else:

                    @pl.loop(0, 1 << left, unroll=2)
                    def _(e):
                        ix = digits(e, left)
                        parts[t][r][(j % 2, which) + tuple(ix)] = total(ix).astype(jnp.bfloat16)

                    send(which, t + 1, r, j).start()

    steps = [(0, project), (1, combine)]
    for t in range(stages):
        steps.append((2 + t, functools.partial(reduce_stage, t)))
    return steps


def gather_scratch(plan, room, tok_rows, units):
    def bf(*shape):
        return pltpu.VMEM(shape, jnp.bfloat16)

    def f32(*shape):
        return pltpu.VMEM(shape, jnp.float32)

    def dma(*shape):
        return pltpu.SemaphoreType.DMA(shape)

    blocks = plan.blocks
    side = blocks // 2
    slot_rows = blocks * room
    landing = [
        bf(LONG_RING, *((2,) * plan.stages), tok_rows, LANES),
        bf(LONG_RING, 3, side, room, LANES),
    ]
    local = [
        bf(2, side, 4 * room, tok_rows),
        f32(slot_rows, LANES),
        bf(3, side, room, LANES),
        bf(3, 3, side, room, LANES),
        bf(2 * slot_rows, 2 * LANES),
        f32(2 * slot_rows, 2 * units),
        bf(3, 2 * LANES, 2 * units),
    ]
    sems = [dma(3, 3), dma(LONG_RING, 3), dma(3, 2)]
    for _ in range(plan.stages):
        sems += [dma(RING, 2), dma(RING, 2)]
    return landing, local, sems


def gather_steps(plan, seg, me, x, places, gates, gains, w_in, act, scratch, sems):
    (held, got, picks, scale, keep, give, lhs, hid, w_buf) = scratch
    blocks = plan.blocks
    side = blocks // 2
    mine = [bit_of(me, bit) for bit in range(plan.count)]
    tok_rows, half = x.shape
    split = plan.split(tok_rows)
    spans = (pl.ds(0, split[0]), pl.ds(split[0], split[1]))
    wide = LANES
    room = keep.shape[-2]
    slot_rows = blocks * room
    units = act.shape[1]
    tile = math.gcd(slot_rows, 256)

    def columns(j):
        return pl.ds(pl.multiple_of(j * wide, wide), wide)

    def send(which, t, r, j):
        order = plan.rest[which][r]
        bit = order[plan.stages - 1 - t]
        free = order[plan.stages - t :]
        rows = spans[r]
        index = tuple(slice(None) if d in free else mine[d] for d in plan.dims(which, r, 0))
        dst = held.at[(j % LONG_RING,) + index + (rows,)]
        return remote(
            x.at[rows, columns(j)] if t == 0 else dst,
            dst,
            sems[3 + 2 * t].at[j % RING, r],
            sems[4 + 2 * t].at[j % RING, r],
            (seg, flip(me, bit)),
        )

    def first_send(which, j):
        for r in range(2):
            send(which, 0, r, j).start()
        index = tuple(mine[d] for d in plan.dims(which, 0, 0))
        held[(j % LONG_RING,) + index] = x[:, columns(j)]

    def relay(t, which, j):
        for r in range(2):
            send(which, t - 1, r, j).wait()
            send(which, t, r, j).start()

    def last_copies(which, j):
        nbr = flip(me, plan.leaf[which])
        peers = ((1 - seg, me), (seg, nbr), (1 - seg, nbr))
        return [
            remote(
                give.at[j % 3, k],
                got.at[j % LONG_RING, k],
                sems[0].at[j % 3, k],
                sems[1].at[j % LONG_RING, k],
                peer,
            )
            for k, peer in enumerate(peers)
        ]

    def weight_copies(j):
        copies = []
        for which, owner in enumerate((seg, 1 - seg)):
            rows = pl.ds(pl.multiple_of(owner * half + j * wide, wide), wide)
            copies.append(
                pltpu.make_async_copy(
                    w_in.at[rows, :],
                    w_buf.at[j % 3, pl.ds(which * wide, wide)],
                    sems[2].at[j % 3, which],
                )
            )
        return copies

    row = lax.broadcasted_iota(jnp.int32, (room, tok_rows), 0).astype(jnp.float32)

    def read_places():
        for which in range(2):
            bit = plan.leaf[which]

            @pl.loop(0, side)
            def _(q):
                d = spread_index(q, bit, mine[bit])
                place = places[d]
                picks[which, q] = jnp.concatenate(
                    [jnp.where(place[k : k + 1, :] == row, 1.0, 0.0) for k in rows_of(which)],
                    axis=0,
                ).astype(jnp.bfloat16)

    def read_factors():
        @pl.loop(0, blocks)
        def _(d):
            own = places[d][0:1, :] == row
            line = gates[d][FACTOR_ROW : FACTOR_ROW + 1, :]
            factor = jnp.sum(jnp.where(own, line, 0.0), axis=1, keepdims=True)
            rows = pl.ds(pl.multiple_of(d * room, room), room)
            scale[rows, :] = jnp.broadcast_to(factor, (room, wide))

    def pick(which, j):
        for copy in weight_copies(j):
            copy.start()
        for r in range(2):
            send(which, plan.stages - 1, r, j).wait()

        @pl.loop(0, side, unroll=4)
        def _(q):
            there = held[(j % LONG_RING,) + tuple(digits(q, plan.stages))]
            taken = jnp.dot(picks[which, q], there, preferred_element_type=jnp.float32)
            taken = taken.astype(jnp.bfloat16)
            keep[j % 3, q] = taken[:room]
            for k in range(3):
                give[j % 3, k, q] = taken[(k + 1) * room : (k + 2) * room]

        for copy in last_copies(which, j):
            copy.start()

    def multiply(which, j):
        for copy in last_copies(which, j):
            copy.wait()
        for copy in weight_copies(j):
            copy.wait()
        bit = plan.leaf[which]
        places = [
            pl.ds(pl.multiple_of(owner * half + j * wide, wide), wide) for owner in (seg, 1 - seg)
        ]
        factors = [[gains[pl.ds(section, 1), place] for place in places] for section in range(2)]

        @pl.loop(0, side, unroll=2)
        def _(q):
            for own, sources in (
                (mine[bit], (keep.at[j % 3, q], got.at[j % LONG_RING, 0, q])),
                (1 - mine[bit], (got.at[j % LONG_RING, 1, q], got.at[j % LONG_RING, 2, q])),
            ):
                base = spread_index(q, bit, own) * room
                factor = scale[pl.ds(pl.multiple_of(base, room), room), :]
                for f, source in enumerate(sources):
                    scaled = source[...].astype(jnp.float32) * factor
                    for section in range(2):
                        to = pl.ds(pl.multiple_of(section * slot_rows + base, room), room)
                        lhs[to, pl.ds(f * wide, wide)] = (scaled * factors[section][f]).astype(
                            jnp.bfloat16
                        )

        for section in range(2):
            rows = pl.ds(section * slot_rows, slot_rows)
            hid[rows, :] += jnp.dot(
                lhs[rows, :], w_buf[j % 3], preferred_element_type=jnp.float32
            )

    def clear():
        @pl.loop(0, 2 * slot_rows // tile)
        def _(r):
            rows = pl.ds(pl.multiple_of(r * tile, tile), tile)
            hid[rows, :] = jnp.zeros((tile, 2 * units), jnp.float32)

    def activate():
        @pl.loop(0, 2 * slot_rows // tile)
        def _(r):
            rows = pl.ds(pl.multiple_of(r * tile, tile), tile)
            gate = hid[rows, :units]
            act[rows, :] = (gate / (1.0 + jnp.exp(-gate)) * hid[rows, units:]).astype(jnp.bfloat16)

    steps = [(0, by_parity(first_send))]
    for t in range(1, plan.stages):
        steps.append((t, by_parity(functools.partial(relay, t))))
    steps += [(plan.stages, by_parity(pick)), (plan.stages + 2, by_parity(multiply))]
    return steps, read_places, read_factors, clear, activate


def column_sum(values):
    return jnp.sum(values, axis=1, keepdims=True)


def fused_kernel(plan, room, capacity, sizes, *refs):
    (x, gain, gain2, ids, copies, later_ids, table, router_in, router2_in, w_in, w_out) = refs[:11]
    states, ratio = refs[11:13]
    n_own, n_gather, n_back, n_gather_sems = sizes
    own = refs[13 : 13 + n_own]
    whole, gain_got, gains, act, mixed, squares, normed, score, score_got = own[:9]
    router, router2, spots, weights, places, gates, wide, w_ring = own[9:]
    refs = refs[13 + n_own :]
    gather_landing, refs = refs[:n_gather], refs[n_gather:]
    back, sems = refs[:n_back], refs[n_back:]
    swap_sems, load_sems, share_sems, sems = sems[:2], sems[2], sems[3:5], sems[5:]
    gather_sems, return_sems = sems[:n_gather_sems], sems[n_gather_sems:]
    seg = lax.axis_index("segment")
    me = lax.axis_index("expert")
    mine = [bit_of(me, bit) for bit in range(plan.count)]
    blocks = plan.blocks
    count = plan.count
    tok_rows, half = x.shape
    full = 2 * half
    top = ids.shape[0]
    tiles = full // LANES
    slot_count = table.shape[1]
    f32 = jnp.float32
    partner = (1 - seg, me)
    at_home = tuple(reversed(mine))

    def tile_at(i):
        return pl.ds(pl.multiple_of(i * LANES, LANES), LANES)

    own_columns = pl.ds(pl.multiple_of(seg * half, half), half)
    swap_x = remote(x, whole.at[:, own_columns], swap_sems[0].at[0], swap_sems[1].at[0], partner)
    swap_gain = remote(gain, gain_got, swap_sems[0].at[1], swap_sems[1].at[1], partner)
    swap_score = remote(score, score_got, swap_sems[0].at[2], swap_sems[1].at[2], partner)
    load_router = pltpu.make_async_copy(router_in, router, load_sems.at[0])
    load_router2 = pltpu.make_async_copy(router2_in, router2, load_sems.at[1])

    def load_w_out(j):
        columns = pl.ds(pl.multiple_of(j * 2 * LANES, 2 * LANES), 2 * LANES)
        return pltpu.make_async_copy(
            w_out.at[:, columns], w_ring.at[j % 3], load_sems.at[2 + j % 3]
        )

    back_chunks = full // (2 * LANES)

    def weight_of(j):
        load_w_out(j).wait()

        @pl.when(j + 2 < back_chunks)
        def _():
            load_w_out(j + 2).start()

        return w_ring.at[j % 3]

    def share(kind, bit):
        ref = (spots, weights)[kind]
        index = tuple(slice(None) if d < bit else mine[d] for d in reversed(range(count)))
        return remote(
            ref.at[index],
            ref.at[index],
            share_sems[0].at[kind, bit],
            share_sems[1].at[kind, bit],
            (seg, flip(me, bit)),
        )

    def matches():
        line = table[...].astype(f32)
        i_row = lax.broadcasted_iota(jnp.int32, (slot_count, slot_count), 0)
        i_col = lax.broadcasted_iota(jnp.int32, (slot_count, slot_count), 1)
        column = column_sum(jnp.where(i_row == i_col, line, 0.0))
        same = column == line
        rank = column_sum(jnp.where(same & (i_col < i_row), 1.0, 0.0))
        holders = column_sum(jnp.where(same, 1.0, 0.0))
        wanted = ids[...].astype(f32)
        choice = copies[...].astype(f32)
        of_two = choice - 2.0 * jnp.floor(choice * 0.5)
        of_three = choice - 3.0 * jnp.floor((choice + 0.5) * (1.0 / 3.0))
        found = []
        for k in range(top):
            turn = jnp.where(
                holders == 1.0,
                0.0,
                jnp.where(holders == 2.0, of_two[k : k + 1, :], of_three[k : k + 1, :]),
            )
            found.append((column == wanted[k : k + 1, :]) & (rank == turn))
        return wanted, found

    def place_tokens():
        hit = jnp.zeros((slot_count, tok_rows), f32)
        for match in matches()[1]:
            hit += jnp.where(match, 1.0, 0.0)
        t_row = lax.broadcasted_iota(jnp.int32, (tok_rows, tok_rows), 0)
        t_col = lax.broadcasted_iota(jnp.int32, (tok_rows, tok_rows), 1)
        earlier = jnp.where(t_row < t_col, 1.0, 0.0).astype(jnp.bfloat16)
        before = jnp.dot(hit.astype(jnp.bfloat16), earlier, preferred_element_type=f32)
        place = jnp.where((hit > 0.0) & (before < capacity), before, -1.0)
        spots[at_home] = place.astype(jnp.bfloat16)

    def normalize():
        total = jnp.zeros((tok_rows, LANES), f32)
        for i in range(tiles):
            part = whole[:, i * LANES : (i + 1) * LANES].astype(f32)
            total += part * part
        return lax.rsqrt(column_sum(total) / full + EPS)

    def prologue():
        gains[1:2, :] = gain[...].astype(f32)
        swap_gain.wait()
        gains[0:1, :] = gain_got[...].astype(f32)
        swap_x.wait()
        squares[...] = jnp.broadcast_to(normalize(), (tok_rows, LANES))

        @pl.loop(0, tiles)
        def _(i):
            part = whole[:, tile_at(i)].astype(f32) * squares[...]
            normed[:, tile_at(i)] = (part * gains[1:2, tile_at(i)]).astype(jnp.bfloat16)

    def weigh_tokens():
        load_router.wait()
        logits = lax.dot_general(
            router[...], normed[...], (((1,), (1,)), ((), ())), preferred_element_type=f32
        )
        names = lax.broadcasted_iota(jnp.int32, logits.shape, 0).astype(f32)
        wanted, found = matches()
        chosen = [
            jnp.sum(jnp.where(names == wanted[k : k + 1, :], logits, 0.0), axis=0, keepdims=True)
            for k in range(top)
        ]
        most = functools.reduce(jnp.maximum, chosen)
        lifted = [jnp.exp(value - most) for value in chosen]
        weight = functools.reduce(jnp.add, lifted)
        gate = jnp.zeros((slot_count, tok_rows), f32)
        for k in range(top):
            rounded = (lifted[k] / weight).astype(jnp.bfloat16).astype(f32)
            gate += jnp.where(found[k], rounded, 0.0)
        rest = squares[...].T[0:1, :]
        rows = [gate]
        for _ in range(3):
            rows.append(rest.astype(jnp.bfloat16).astype(f32))
            rest = rest - rows[-1]
        rows.append(jnp.zeros((EXTRA_ROWS - 3, tok_rows), f32))
        weights[at_home] = jnp.concatenate(rows, axis=0).astype(jnp.bfloat16)

    def widen(kind):
        source, target = (spots, weights)[kind], (places, gates)[kind]

        @pl.loop(0, blocks)
        def _(d):
            wide[kind, : source.shape[-2]] = source[tuple(digits(d, count))].astype(f32)
            for k, slot in enumerate(slots_of(plan, seg, me)):
                target[d, k : k + 1, :] = wide[kind, pl.ds(slot, 1), :]
            if kind == 1:
                extra = wide[kind, slot_count : slot_count + 8, :]
                target[d, FACTOR_ROW : FACTOR_ROW + 1, :] = jnp.sum(extra, axis=0, keepdims=True)

    def pass_on(when):
        if when == 0:
            prologue()
        if when == 1:
            weigh_tokens()
            share(1, 0).start()
        if when <= count - 2:
            share(0, when).wait()
            share(0, when + 1).start()
        if 2 <= when <= count:
            share(1, when - 2).wait()
            share(1, when - 1).start()

    def combine_weights():
        make_weights(plan, me, room, places, gates, back[0])

    def gather_part(*local):
        steps, read_places, read_factors, clear, activate = gather_steps(
            plan, seg, me, x, places, gates, gains, w_in, act, gather_landing + local, gather_sems
        )

        def take_places():
            share(0, count - 1).wait()
            widen(0)
            read_places()

        def take_factors():
            share(1, count - 1).wait()
            widen(1)
            read_factors()

        place_tokens()
        whole[:, own_columns] = x[...]
        clear()
        pl.semaphore_wait(barrier, len(friends))
        swap_x.start()
        swap_gain.start()
        share(0, 0).start()
        late = {when: functools.partial(pass_on, when) for when in range(count + 1)}
        late[count + 3] = combine_weights
        early = {plan.stages: take_places, plan.stages + 2: take_factors}
        run_stages(half // LANES, steps, early, late)
        activate()

    def finish(rows, columns, total):
        value = whole[rows, columns].astype(f32) + total
        mixed[rows, columns] = value
        states[rows, columns] = value.astype(jnp.bfloat16)
        squares[rows, :] += value * value

    def return_part(*local):
        steps = return_steps(plan, seg, me, act, weight_of, finish, back, local, return_sems)
        run_stages(back_chunks, steps, {}, {})

    barrier = pltpu.get_barrier_semaphore()
    friends = near_friends(plan, seg, me)
    for friend in friends:
        pl.semaphore_signal(barrier, inc=1, device_id=friend, device_id_type=MESH)
    load_router.start()
    load_router2.start()
    load_w_out(0).start()
    load_w_out(1).start()
    pl.run_scoped(gather_part, *gather_scratch(plan, room, tok_rows, act.shape[1])[1])
    squares[...] = jnp.zeros((tok_rows, LANES), f32)
    pl.run_scoped(return_part, *return_scratch(plan, room, tok_rows)[1])
    inverse = lax.rsqrt(column_sum(squares[...]) / full + EPS)
    squares[...] = jnp.broadcast_to(inverse, (tok_rows, LANES))

    @pl.loop(0, tiles)
    def _(i):
        part = mixed[:, tile_at(i)] * squares[...]
        normed[:, tile_at(i)] = (part * gain2[:, tile_at(i)].astype(f32)).astype(jnp.bfloat16)

    load_router2.wait()
    logits = lax.dot_general(
        router2[...], normed[...], (((1,), (1,)), ((), ())), preferred_element_type=f32
    )
    shifted = logits - jnp.max(logits, axis=0, keepdims=True)
    logp = shifted - jnp.log(jnp.sum(jnp.exp(shifted), axis=0, keepdims=True))
    names = lax.broadcasted_iota(jnp.int32, logits.shape, 0).astype(f32)
    wanted = later_ids[...].astype(f32)
    total = jnp.zeros((1, tok_rows), f32)
    for k in range(top):
        total += jnp.sum(jnp.where(names == wanted[k : k + 1, :], logp, 0.0), axis=0, keepdims=True)
    score[...] = jnp.broadcast_to(total, score.shape)
    swap_score.start()
    swap_score.wait()
    sign = (2 * seg - 1).astype(f32)
    difference = (score[0:1, :] - score_got[0:1, :]) * sign
    turned = jnp.broadcast_to(difference, (tok_rows, tok_rows)).T
    t_row = lax.broadcasted_iota(jnp.int32, (tok_rows, tok_rows), 0)
    t_col = lax.broadcasted_iota(jnp.int32, (tok_rows, tok_rows), 1)
    picked = jnp.sum(jnp.where(t_row == 2 * t_col + seg, turned, 0.0), axis=0, keepdims=True)
    ratio[...] = picked[:, : tok_rows // 2]


def fused_scratch(plan, room, tok_rows, half, slot_count, units, experts):
    full = 2 * half
    rows = 2 * plan.blocks * room
    low = (2,) * plan.count

    def bf(*shape):
        return pltpu.VMEM(shape, jnp.bfloat16)

    def f32(*shape):
        return pltpu.VMEM(shape, jnp.float32)

    own = [
        bf(tok_rows, full),
        bf(1, full),
        f32(2, full),
        bf(rows, units),
        f32(tok_rows, full),
        f32(tok_rows, LANES),
        bf(tok_rows, full),
        f32(8, tok_rows),
        f32(8, tok_rows),
        bf(experts, full),
        bf(experts, full),
        bf(*low, slot_count, tok_rows),
        bf(*low, slot_count + EXTRA_ROWS, tok_rows),
        f32(plan.blocks, 8, tok_rows),
        f32(plan.blocks, 8, tok_rows),
        f32(2, slot_count + EXTRA_ROWS, tok_rows),
        bf(3, units, 2 * LANES),
    ]
    gather, _, gather_sems = gather_scratch(plan, room, tok_rows, units)
    back, _, back_sems = return_scratch(plan, room, tok_rows)
    shapes = ((3,), (3,), (5,), (2, plan.count), (2, plan.count))
    swap = [pltpu.SemaphoreType.DMA(shape) for shape in shapes]
    sizes = (len(own), len(gather), len(back), len(gather_sems))
    return own + gather + back, swap + gather_sems + back_sems, sizes


def fused_call(plan, room, capacity, scratch, sems, sizes, *args):
    tok_rows, half = args[0].shape
    vmem = pl.BlockSpec(memory_space=pltpu.VMEM)
    anywhere = pl.BlockSpec(memory_space=pl.ANY)
    return pl.pallas_call(
        functools.partial(fused_kernel, plan, room, capacity, sizes),
        out_shape=(
            jax.ShapeDtypeStruct((tok_rows, 2 * half), jnp.bfloat16),
            jax.ShapeDtypeStruct((1, tok_rows // 2), jnp.float32),
        ),
        in_specs=[vmem] * 7 + [anywhere] * 4,
        out_specs=(vmem, vmem),
        scratch_shapes=scratch + sems,
        compiler_params=pltpu.CompilerParams(
            collective_id=0, has_side_effects=True, vmem_limit_bytes=VMEM_MOST
        ),
        name="fused_layer",
    )(*args)


def per_device(
    rollout,
    norm_gain,
    router_first,
    gain_second,
    router_second,
    expert_ids,
    copy_pick,
    later_ids,
    slot_table,
    expert_in,
    expert_out,
):
    segment_count = lax.axis_size("segment")
    chip_count = lax.axis_size("expert")
    tok_rows, half = rollout.shape
    capacity = 3 * tok_rows * expert_ids.shape[1] // (2 * segment_count * chip_count)
    plan = Plan(grid_sides(chip_count))
    room = -(-capacity // 16) * 16
    scratch, sems, sizes = fused_scratch(
        plan,
        room,
        tok_rows,
        half,
        slot_table.shape[0],
        expert_out.shape[1],
        router_first.shape[2],
    )
    states, column = fused_call(
        plan,
        room,
        capacity,
        scratch,
        sems,
        sizes,
        rollout,
        norm_gain,
        gain_second,
        expert_ids.T,
        copy_pick.T,
        later_ids.T,
        slot_table[None, :],
        router_first[0].T,
        router_second[0].T,
        expert_in[0],
        expert_out[0],
    )
    return states[None], column.reshape(-1, 1)


def solution(mesh):
    in_specs = (
        P("expert", "segment"),
        P("segment", None),
        P("segment", None, None),
        P("segment", None),
        P("segment", None, None),
        P("expert", None),
        P("expert", None),
        P("expert", None),
        P(),
        P(("segment", "expert"), None, None),
        P(("segment", "expert"), None, None),
    )
    out_specs = (P("segment", "expert", None), P("expert", "segment"))
    return jax.shard_map(
        per_device, mesh=mesh, in_specs=in_specs, out_specs=out_specs, check_vma=False
    )
```

time: 209 us -> 208 us (level)
  no operation moved by 1% of the time
where the time goes in v2:
time: 208 us
  Pallas kernels  204 us (98%)
  local copies, waits for them, and re-layouts  3.4 us (2%)
    pallas_call x1, Pallas kernels, fused_call(): pl.pallas_call(functools.partial(fused_kernel, plan, room, capacity, size...  204 us

profile of v2, /device:TPU:0, one launch (start us, length us, event | category | flops | bytes accessed | tf_op | source)
XLA Modules:
  0.0 207.6 jit_solution(17897646244636140923)
XLA Ops:
  0.6 203.6 %fused_layer.1 = (bf16[128,4096]{1,0:T(8,128)(2,1)}, f32[1,64]{1,0:T(1,128)}) custom-call(bf16[128,2048]{1,0:T(8,128)(2,1)} %refs_0_.1, bf16[1,4096]{1,0:T(2,128)(2,1)} %refs_1_.1, bf16[1,4096]{1,0:T(2,128)(2,1)} %refs_2_.1, s32[8,128]{1,0:T(8,128)} %bitcast.19, s32[8,128]{1,0:T(8,128)} %bitcast.20, s32[8,128]{1,0:T(8,128)} %bitcast.21, s32[1,32]{1,0:T(1,128)} %bitcast.22, ...), custom_call_target="tpu_custom_call" | custom-call | tf_op jit(solution)/shard_map/fused_layer/pallas_call | solution.py:808
  204.2 2.3 %copy.15 = bf16[1,128,4096]{2,1,0:T(8,128)(2,1)} copy(bf16[1,128,4096]{2,1,0:T(8,128)(2,1)} %bitcast.16) | data formatting | bytes 2097152
  206.5 1.1 copy.16

commit v3 on v2

--- a/solution.py
+++ b/solution.py
@@ -13,10 +13,7 @@
 MESH = pl.DeviceIdType.MESH
 EPS = 1e-06
 RING = 4
-LONG_RING = 8
 EXTRA_ROWS = 16
-NEAR_SLOTS = 6
-FACTOR_ROW = 6
 
 
 def grid_sides(count):
@@ -46,6 +43,17 @@
         )
         self.rest = [[order[1:] for order in pair] for pair in orders]
         self.stages = self.count - 1
+        self.gap = 2 if self.count <= 4 else 1
+        self.last_gap = self.gap + 1
+        self.pick_lag = self.gap * self.stages
+        self.multiply_lag = self.pick_lag + self.last_gap
+        self.stage_ring = self.ring(self.gap, self.gap)
+        self.held_ring = self.ring(self.pick_lag, self.gap)
+        self.last_ring = self.ring(self.last_gap, self.last_gap)
+
+    def ring(self, busy, gap):
+        ahead = busy + 1 + (busy + 1) % 2
+        return ahead + 1 + gap + (ahead + 1 + gap) % 2
 
     def split(self, rows):
         part = max(3 * rows // 8 // 16 * 16, 16)
@@ -325,37 +333,39 @@
     blocks = plan.blocks
     side = blocks // 2
     slot_rows = blocks * room
+    near = plan.last_gap + 1
     landing = [
-        bf(LONG_RING, *((2,) * plan.stages), tok_rows, LANES),
-        bf(LONG_RING, 3, side, room, LANES),
+        bf(plan.held_ring, *((2,) * plan.stages), tok_rows, LANES),
+        bf(plan.last_ring, 3, side, room, LANES),
     ]
     local = [
         bf(2, side, 4 * room, tok_rows),
         f32(slot_rows, LANES),
-        bf(3, side, room, LANES),
-        bf(3, 3, side, room, LANES),
+        bf(near, side, room, LANES),
+        bf(near, 3, side, room, LANES),
         bf(2 * slot_rows, 2 * LANES),
         f32(2 * slot_rows, 2 * units),
-        bf(3, 2 * LANES, 2 * units),
+        bf(near, 2 * LANES, 2 * units),
     ]
-    sems = [dma(3, 3), dma(LONG_RING, 3), dma(3, 2)]
+    sems = [dma(near, 3), dma(plan.last_ring, 3), dma(near, 2)]
     for _ in range(plan.stages):
-        sems += [dma(RING, 2), dma(RING, 2)]
+        sems += [dma(plan.stage_ring, 2), dma(plan.stage_ring, 2)]
     return landing, local, sems
 
 
-def gather_steps(plan, seg, me, x, places, gates, gains, w_in, act, scratch, sems):
+def gather_steps(plan, seg, me, x, places, squares, gains, w_in, act, scratch, sems):
     (held, got, picks, scale, keep, give, lhs, hid, w_buf) = scratch
     blocks = plan.blocks
     side = blocks // 2
     mine = [bit_of(me, bit) for bit in range(plan.count)]
     tok_rows, half = x.shape
-    split = plan.split(tok_rows)
+    split = (tok_rows // 2, tok_rows // 2)
     spans = (pl.ds(0, split[0]), pl.ds(split[0], split[1]))
     wide = LANES
     room = keep.shape[-2]
     slot_rows = blocks * room
     units = act.shape[1]
+    near = plan.last_gap + 1
     tile = math.gcd(slot_rows, 256)
 
     def columns(j):
@@ -367,12 +377,12 @@
         free = order[plan.stages - t :]
         rows = spans[r]
         index = tuple(slice(None) if d in free else mine[d] for d in plan.dims(which, r, 0))
-        dst = held.at[(j % LONG_RING,) + index + (rows,)]
+        dst = held.at[(j % plan.held_ring,) + index + (rows,)]
         return remote(
             x.at[rows, columns(j)] if t == 0 else dst,
             dst,
-            sems[3 + 2 * t].at[j % RING, r],
-            sems[4 + 2 * t].at[j % RING, r],
+            sems[3 + 2 * t].at[j % plan.stage_ring, r],
+            sems[4 + 2 * t].at[j % plan.stage_ring, r],
             (seg, flip(me, bit)),
         )
 
@@ -380,7 +390,7 @@
         for r in range(2):
             send(which, 0, r, j).start()
         index = tuple(mine[d] for d in plan.dims(which, 0, 0))
-        held[(j % LONG_RING,) + index] = x[:, columns(j)]
+        held[(j % plan.held_ring,) + index] = x[:, columns(j)]
 
     def relay(t, which, j):
         for r in range(2):
@@ -392,10 +402,10 @@
         peers = ((1 - seg, me), (seg, nbr), (1 - seg, nbr))
         return [
             remote(
-                give.at[j % 3, k],
-                got.at[j % LONG_RING, k],
-                sems[0].at[j % 3, k],
-                sems[1].at[j % LONG_RING, k],
+                give.at[j % near, k],
+                got.at[j % plan.last_ring, k],
+                sems[0].at[j % near, k],
+                sems[1].at[j % plan.last_ring, k],
                 peer,
             )
             for k, peer in enumerate(peers)
@@ -408,8 +418,8 @@
             copies.append(
                 pltpu.make_async_copy(
                     w_in.at[rows, :],
-                    w_buf.at[j % 3, pl.ds(which * wide, wide)],
-                    sems[2].at[j % 3, which],
+                    w_buf.at[j % near, pl.ds(which * wide, wide)],
+                    sems[2].at[j % near, which],
                 )
             )
         return copies
@@ -433,7 +443,8 @@
         @pl.loop(0, blocks)
         def _(d):
             own = places[d][0:1, :] == row
-            line = gates[d][FACTOR_ROW : FACTOR_ROW + 1, :]
+            total = squares[0, pl.ds(d, 1), :] + squares[1, pl.ds(d, 1), :]
+            line = lax.rsqrt(total / (2 * half) + EPS)
             factor = jnp.sum(jnp.where(own, line, 0.0), axis=1, keepdims=True)
             rows = pl.ds(pl.multiple_of(d * room, room), room)
             scale[rows, :] = jnp.broadcast_to(factor, (room, wide))
@@ -444,14 +455,14 @@
         for r in range(2):
             send(which, plan.stages - 1, r, j).wait()
 
-        @pl.loop(0, side, unroll=4)
+        @pl.loop(0, side, unroll=8)
         def _(q):
-            there = held[(j % LONG_RING,) + tuple(digits(q, plan.stages))]
+            there = held[(j % plan.held_ring,) + tuple(digits(q, plan.stages))]
             taken = jnp.dot(picks[which, q], there, preferred_element_type=jnp.float32)
             taken = taken.astype(jnp.bfloat16)
-            keep[j % 3, q] = taken[:room]
+            keep[j % near, q] = taken[:room]
             for k in range(3):
-                give[j % 3, k, q] = taken[(k + 1) * room : (k + 2) * room]
+                give[j % near, k, q] = taken[(k + 1) * room : (k + 2) * room]
 
         for copy in last_copies(which, j):
             copy.start()
@@ -470,8 +481,8 @@
         @pl.loop(0, side, unroll=2)
         def _(q):
             for own, sources in (
-                (mine[bit], (keep.at[j % 3, q], got.at[j % LONG_RING, 0, q])),
-                (1 - mine[bit], (got.at[j % LONG_RING, 1, q], got.at[j % LONG_RING, 2, q])),
+                (mine[bit], (keep.at[j % near, q], got.at[j % plan.last_ring, 0, q])),
+                (1 - mine[bit], (got.at[j % plan.last_ring, 1, q], got.at[j % plan.last_ring, 2, q])),
             ):
                 base = spread_index(q, bit, own) * room
                 factor = scale[pl.ds(pl.multiple_of(base, room), room), :]
@@ -486,7 +497,7 @@
         for section in range(2):
             rows = pl.ds(section * slot_rows, slot_rows)
             hid[rows, :] += jnp.dot(
-                lhs[rows, :], w_buf[j % 3], preferred_element_type=jnp.float32
+                lhs[rows, :], w_buf[j % near], preferred_element_type=jnp.float32
             )
 
     def clear():
@@ -504,8 +515,8 @@
 
     steps = [(0, by_parity(first_send))]
     for t in range(1, plan.stages):
-        steps.append((t, by_parity(functools.partial(relay, t))))
-    steps += [(plan.stages, by_parity(pick)), (plan.stages + 2, by_parity(multiply))]
+        steps.append((plan.gap * t, by_parity(functools.partial(relay, t))))
+    steps += [(plan.pick_lag, by_parity(pick)), (plan.multiply_lag, by_parity(multiply))]
     return steps, read_places, read_factors, clear, activate
 
 
@@ -519,7 +530,7 @@
     n_own, n_gather, n_back, n_gather_sems = sizes
     own = refs[13 : 13 + n_own]
     whole, gain_got, gains, act, mixed, squares, normed, score, score_got = own[:9]
-    router, router2, spots, weights, places, gates, wide, w_ring = own[9:]
+    router, router2, spots, weights, places, gates, wide, w_ring, halves = own[9:]
     refs = refs[13 + n_own :]
     gather_landing, refs = refs[:n_gather], refs[n_gather:]
     back, sems = refs[:n_back], refs[n_back:]
@@ -545,6 +556,9 @@
     own_columns = pl.ds(pl.multiple_of(seg * half, half), half)
     swap_x = remote(x, whole.at[:, own_columns], swap_sems[0].at[0], swap_sems[1].at[0], partner)
     swap_gain = remote(gain, gain_got, swap_sems[0].at[1], swap_sems[1].at[1], partner)
+    swap_halves = remote(
+        halves.at[0], halves.at[1], swap_sems[0].at[3], swap_sems[1].at[3], partner
+    )
     swap_score = remote(score, score_got, swap_sems[0].at[2], swap_sems[1].at[2], partner)
     load_router = pltpu.make_async_copy(router_in, router, load_sems.at[0])
     load_router2 = pltpu.make_async_copy(router2_in, router2, load_sems.at[1])
@@ -608,7 +622,17 @@
         earlier = jnp.where(t_row < t_col, 1.0, 0.0).astype(jnp.bfloat16)
         before = jnp.dot(hit.astype(jnp.bfloat16), earlier, preferred_element_type=f32)
         place = jnp.where((hit > 0.0) & (before < capacity), before, -1.0)
-        spots[at_home] = place.astype(jnp.bfloat16)
+        total = jnp.zeros((tok_rows, LANES), f32)
+        for i in range(half // LANES):
+            part = x[:, i * LANES : (i + 1) * LANES].astype(f32)
+            total += part * part
+        rest = jnp.broadcast_to(column_sum(total), (tok_rows, LANES)).T[0:1, :]
+        rows = [place]
+        for _ in range(3):
+            rows.append(rest.astype(jnp.bfloat16).astype(f32))
+            rest = rest - rows[-1]
+        rows.append(jnp.zeros((EXTRA_ROWS - 3, tok_rows), f32))
+        spots[at_home] = jnp.concatenate(rows, axis=0).astype(jnp.bfloat16)
 
     def normalize():
         total = jnp.zeros((tok_rows, LANES), f32)
@@ -618,9 +642,6 @@
         return lax.rsqrt(column_sum(total) / full + EPS)
 
     def prologue():
-        gains[1:2, :] = gain[...].astype(f32)
-        swap_gain.wait()
-        gains[0:1, :] = gain_got[...].astype(f32)
         swap_x.wait()
         squares[...] = jnp.broadcast_to(normalize(), (tok_rows, LANES))
 
@@ -647,13 +668,7 @@
         for k in range(top):
             rounded = (lifted[k] / weight).astype(jnp.bfloat16).astype(f32)
             gate += jnp.where(found[k], rounded, 0.0)
-        rest = squares[...].T[0:1, :]
-        rows = [gate]
-        for _ in range(3):
-            rows.append(rest.astype(jnp.bfloat16).astype(f32))
-            rest = rest - rows[-1]
-        rows.append(jnp.zeros((EXTRA_ROWS - 3, tok_rows), f32))
-        weights[at_home] = jnp.concatenate(rows, axis=0).astype(jnp.bfloat16)
+        weights[at_home] = gate.astype(jnp.bfloat16)
 
     def widen(kind):
         source, target = (spots, weights)[kind], (places, gates)[kind]
@@ -663,51 +678,58 @@
             wide[kind, : source.shape[-2]] = source[tuple(digits(d, count))].astype(f32)
             for k, slot in enumerate(slots_of(plan, seg, me)):
                 target[d, k : k + 1, :] = wide[kind, pl.ds(slot, 1), :]
-            if kind == 1:
+            if kind == 0:
                 extra = wide[kind, slot_count : slot_count + 8, :]
-                target[d, FACTOR_ROW : FACTOR_ROW + 1, :] = jnp.sum(extra, axis=0, keepdims=True)
-
-    def pass_on(when):
-        if when == 0:
-            prologue()
-        if when == 1:
-            weigh_tokens()
-            share(1, 0).start()
-        if when <= count - 2:
-            share(0, when).wait()
-            share(0, when + 1).start()
-        if 2 <= when <= count:
-            share(1, when - 2).wait()
-            share(1, when - 1).start()
+                halves[0, pl.ds(d, 1), :] = jnp.sum(extra, axis=0, keepdims=True)
+
+    def pass_on(kind, bit):
+        if bit:
+            share(kind, bit - 1).wait()
+        share(kind, bit).start()
 
     def combine_weights():
+        share(1, count - 1).wait()
+        widen(1)
         make_weights(plan, me, room, places, gates, back[0])
+
+    def begin_weights():
+        weigh_tokens()
+        pass_on(1, 0)
 
     def gather_part(*local):
         steps, read_places, read_factors, clear, activate = gather_steps(
-            plan, seg, me, x, places, gates, gains, w_in, act, gather_landing + local, gather_sems
+            plan, seg, me, x, places, halves, gains, w_in, act, gather_landing + local, gather_sems
         )
 
         def take_places():
             share(0, count - 1).wait()
             widen(0)
+            swap_halves.start()
             read_places()
 
         def take_factors():
-            share(1, count - 1).wait()
-            widen(1)
+            swap_gain.wait()
+            gains[0:1, :] = gain_got[...].astype(f32)
+            swap_halves.wait()
             read_factors()
 
         place_tokens()
         whole[:, own_columns] = x[...]
+        gains[1:2, :] = gain[...].astype(f32)
         clear()
         pl.semaphore_wait(barrier, len(friends))
         swap_x.start()
         swap_gain.start()
         share(0, 0).start()
-        late = {when: functools.partial(pass_on, when) for when in range(count + 1)}
-        late[count + 3] = combine_weights
-        early = {plan.stages: take_places, plan.stages + 2: take_factors}
+        late = {bit - 1: functools.partial(pass_on, 0, bit) for bit in range(1, count)}
+        last = half // LANES + plan.multiply_lag - 1
+        pace = min(3, (last - count) // count)
+        late[count - 1] = prologue
+        late[count] = begin_weights
+        for bit in range(1, count):
+            late[count + pace * bit] = functools.partial(pass_on, 1, bit)
+        late[count + pace * count] = combine_weights
+        early = {plan.pick_lag: take_places, plan.multiply_lag: take_factors}
         run_stages(half // LANES, steps, early, late)
         activate()
 
@@ -786,16 +808,17 @@
         f32(8, tok_rows),
         bf(experts, full),
         bf(experts, full),
+        bf(*low, slot_count + EXTRA_ROWS, tok_rows),
         bf(*low, slot_count, tok_rows),
-        bf(*low, slot_count + EXTRA_ROWS, tok_rows),
         f32(plan.blocks, 8, tok_rows),
         f32(plan.blocks, 8, tok_rows),
         f32(2, slot_count + EXTRA_ROWS, tok_rows),
         bf(3, units, 2 * LANES),
+        f32(2, plan.blocks, tok_rows),
     ]
     gather, _, gather_sems = gather_scratch(plan, room, tok_rows, units)
     back, _, back_sems = return_scratch(plan, room, tok_rows)
-    shapes = ((3,), (3,), (5,), (2, plan.count), (2, plan.count))
+    shapes = ((4,), (4,), (5,), (2, plan.count), (2, plan.count))
     swap = [pltpu.SemaphoreType.DMA(shape) for shape in shapes]
     sizes = (len(own), len(gather), len(back), len(gather_sems))
     return own + gather + back, swap + gather_sems + back_sems, sizes

time: 208 us -> 204 us (0.981)
  Pallas kernels: 204 us -> 199 us
    pallas_call x1, Pallas kernels: 204 us -> 199 us  [fused_call(): pl.pallas_call(functools.partial(fused_kernel, plan, room, capacity, size...]
where the time goes in v3:
time: 204 us
  Pallas kernels  199 us (98%)
  local copies, waits for them, and re-layouts  3.4 us (2%)
    pallas_call x1, Pallas kernels, fused_call(): pl.pallas_call(functools.partial(fused_kernel, plan, room, capacity, size...  199 us

profile of v3, /device:TPU:0, one launch (start us, length us, event | category | flops | bytes accessed | tf_op | source)
XLA Modules:
  0.0 203.5 jit_solution(449680078211970004)
XLA Ops:
  0.6 199.5 %fused_layer.1 = (bf16[128,4096]{1,0:T(8,128)(2,1)}, f32[1,64]{1,0:T(1,128)}) custom-call(bf16[128,2048]{1,0:T(8,128)(2,1)} %refs_0_.1, bf16[1,4096]{1,0:T(2,128)(2,1)} %refs_1_.1, bf16[1,4096]{1,0:T(2,128)(2,1)} %refs_2_.1, s32[8,128]{1,0:T(8,128)} %bitcast.19, s32[8,128]{1,0:T(8,128)} %bitcast.20, s32[8,128]{1,0:T(8,128)} %bitcast.21, s32[1,32]{1,0:T(1,128)} %bitcast.22, ...), custom_call_target="tpu_custom_call" | custom-call | tf_op jit(solution)/shard_map/fused_layer/pallas_call | solution.py:831
  200.1 2.3 %copy.15 = bf16[1,128,4096]{2,1,0:T(8,128)(2,1)} copy(bf16[1,128,4096]{2,1,0:T(8,128)(2,1)} %bitcast.16) | data formatting | bytes 2097152
  202.4 1.1 copy.16

commit v4 on v3

--- a/solution.py
+++ b/solution.py
@@ -13,6 +13,8 @@
 MESH = pl.DeviceIdType.MESH
 EPS = 1e-06
 RING = 4
+GAPS = (3, 3, 3)
+LAST_GAP = 3
 EXTRA_ROWS = 16
 
 
@@ -43,9 +45,12 @@
         )
         self.rest = [[order[1:] for order in pair] for pair in orders]
         self.stages = self.count - 1
-        self.gap = 2 if self.count <= 4 else 1
-        self.last_gap = self.gap + 1
-        self.pick_lag = self.gap * self.stages
+        short = self.stages == len(GAPS)
+        gaps = GAPS if short else (1,) * self.stages
+        self.lags = [sum(gaps[:t]) for t in range(self.stages + 1)]
+        self.gap = max(gaps)
+        self.last_gap = LAST_GAP if short else 2
+        self.pick_lag = self.lags[-1]
         self.multiply_lag = self.pick_lag + self.last_gap
         self.stage_ring = self.ring(self.gap, self.gap)
         self.held_ring = self.ring(self.pick_lag, self.gap)
@@ -515,7 +520,7 @@
 
     steps = [(0, by_parity(first_send))]
     for t in range(1, plan.stages):
-        steps.append((plan.gap * t, by_parity(functools.partial(relay, t))))
+        steps.append((plan.lags[t], by_parity(functools.partial(relay, t))))
     steps += [(plan.pick_lag, by_parity(pick)), (plan.multiply_lag, by_parity(multiply))]
     return steps, read_places, read_factors, clear, activate
 
@@ -721,14 +726,15 @@
         swap_x.start()
         swap_gain.start()
         share(0, 0).start()
-        late = {bit - 1: functools.partial(pass_on, 0, bit) for bit in range(1, count)}
+        late = {plan.lags[bit] - 1: functools.partial(pass_on, 0, bit) for bit in range(1, count)}
         last = half // LANES + plan.multiply_lag - 1
-        pace = min(3, (last - count) // count)
-        late[count - 1] = prologue
-        late[count] = begin_weights
+        start = plan.pick_lag + 2
+        pace = min(3, (last - start) // count)
+        late[start - 1] = prologue
+        late[start] = begin_weights
         for bit in range(1, count):
-            late[count + pace * bit] = functools.partial(pass_on, 1, bit)
-        late[count + pace * count] = combine_weights
+            late[start + pace * bit] = functools.partial(pass_on, 1, bit)
+        late[start + pace * count] = combine_weights
         early = {plan.pick_lag: take_places, plan.multiply_lag: take_factors}
         run_stages(half // LANES, steps, early, late)
         activate()

time: 204 us -> 200 us (0.980)
  Pallas kernels: 199 us -> 196 us
    pallas_call x1, Pallas kernels: 199 us -> 196 us  [fused_call(): pl.pallas_call(functools.partial(fused_kernel, plan, room, capacity, size...]
where the time goes in v4:
time: 200 us
  Pallas kernels  196 us (98%)
  local copies, waits for them, and re-layouts  3.4 us (2%)
    pallas_call x1, Pallas kernels, fused_call(): pl.pallas_call(functools.partial(fused_kernel, plan, room, capacity, size...  196 us

profile of v4, /device:TPU:0, one launch (start us, length us, event | category | flops | bytes accessed | tf_op | source)
XLA Modules:
  0.0 200.3 jit_solution(16481932461671596024)
XLA Ops:
  0.6 196.3 %fused_layer.1 = (bf16[128,4096]{1,0:T(8,128)(2,1)}, f32[1,64]{1,0:T(1,128)}) custom-call(bf16[128,2048]{1,0:T(8,128)(2,1)} %refs_0_.1, bf16[1,4096]{1,0:T(2,128)(2,1)} %refs_1_.1, bf16[1,4096]{1,0:T(2,128)(2,1)} %refs_2_.1, s32[8,128]{1,0:T(8,128)} %bitcast.19, s32[8,128]{1,0:T(8,128)} %bitcast.20, s32[8,128]{1,0:T(8,128)} %bitcast.21, s32[1,32]{1,0:T(1,128)} %bitcast.22, ...), custom_call_target="tpu_custom_call" | custom-call | tf_op jit(solution)/shard_map/fused_layer/pallas_call | solution.py:837
  196.9 2.3 %copy.15 = bf16[1,128,4096]{2,1,0:T(8,128)(2,1)} copy(bf16[1,128,4096]{2,1,0:T(8,128)(2,1)} %bitcast.16) | data formatting | bytes 2097152
  199.2 1.1 copy.16

commit v5 on v4

--- a/solution.py
+++ b/solution.py
@@ -218,7 +218,7 @@
             for i in range(plan.count)
         )
 
-    def first_copies(which, j):
+    def first_copies(which, j, kept=(0, 1, 2)):
         nbr = flip(me, plan.leaf[which])
         sources = (
             (ys.at[(j % 2, which, 1) + region(which, False)], leaf.at[j % RING, which, 0], (seg, nbr)),
@@ -228,6 +228,7 @@
         return [
             remote(src, dst, sems[0].at[j % 2, which, k], sems[1].at[j % RING, which, k], peer)
             for k, (src, dst, peer) in enumerate(sources)
+            if k in kept
         ]
 
     def held_at(which, t, r, j, index):
@@ -260,10 +261,9 @@
             for which in range(2):
                 half = result[:, which * LANES : (which + 1) * LANES]
                 ys[j % 2, which, section] = half.reshape(blocks + (room, LANES))
-        for which in range(2):
-            for copy in first_copies(which, j):
-                copy.start()
-
+            for which in range(2):
+                for k in ((1, 2), (0,))[section]:
+                    first_copies(which, j, (k,))[0].start()
     def combine(j):
         for which in range(2):
             for copy in first_copies(which, j):

time: 200 us -> 200 us (level)
  no operation moved by 1% of the time
where the time goes in v5:
time: 200 us
  Pallas kernels  196 us (98%)
  local copies, waits for them, and re-layouts  3.4 us (2%)
    pallas_call x1, Pallas kernels, fused_call(): pl.pallas_call(functools.partial(fused_kernel, plan, room, capacity, size...  196 us

profile of v5, /device:TPU:0, one launch (start us, length us, event | category | flops | bytes accessed | tf_op | source)
XLA Modules:
  0.0 200.2 jit_solution(10461671952717476598)
XLA Ops:
  0.6 196.2 %fused_layer.1 = (bf16[128,4096]{1,0:T(8,128)(2,1)}, f32[1,64]{1,0:T(1,128)}) custom-call(bf16[128,2048]{1,0:T(8,128)(2,1)} %refs_0_.1, bf16[1,4096]{1,0:T(2,128)(2,1)} %refs_1_.1, bf16[1,4096]{1,0:T(2,128)(2,1)} %refs_2_.1, s32[8,128]{1,0:T(8,128)} %bitcast.19, s32[8,128]{1,0:T(8,128)} %bitcast.20, s32[8,128]{1,0:T(8,128)} %bitcast.21, s32[1,32]{1,0:T(1,128)} %bitcast.22, ...), custom_call_target="tpu_custom_call" | custom-call | tf_op jit(solution)/shard_map/fused_layer/pallas_call | solution.py:837
  196.8 2.3 %copy.15 = bf16[1,128,4096]{2,1,0:T(8,128)(2,1)} copy(bf16[1,128,4096]{2,1,0:T(8,128)(2,1)} %bitcast.16) | data formatting | bytes 2097152
  199.1 1.1 copy.16
